TPU v7x, 32 devices: a whole 2x2x4 slice. The times are simulated.
32 devices in a mesh: space: 4 (over z), energy: 8 (over y, x, core).
Axes of the slice: x: 2, y: 2, z: 4, core: 2. Of those that a mesh axis runs over, the one named last changes fastest.
Arguments:
- retain: float32 [8, 8], P('space', 'energy'), may hold values from 0.12 to 0.89
- hopping: float32 [8, 8, 2, 128, 128], P('space', 'energy'), may hold values from -0.125 to 0.125
- source: float32 [8, 8, 2, 128, 128], P('space', 'energy'), may hold values from -0.9 to 0.9
- screened: float32 [8, 8, 2, 16384], P('space', None, None, 'energy'), may hold values from -2 to 2
Outputs:
- greens: float32 [8, 8, 2, 128, 128], P('space', 'energy')
- self_energy: float32 [8, 8, 2, 16384], P('space', None, None, 'energy')
All inputs are finite; a program needn't handle non-finite values.
Results may differ from a plain program's by a relative error of at most 0.0001.
Values sent between devices are 32-bit elements; how exact they have to be, the bound alone decides.
A program may use at most 64 MiB of HBM per device.

v0:
```python
import functools

import jax
import jax.numpy as jnp
from jax import lax
from jax.experimental import pallas as pl
from jax.experimental.pallas import tpu as pltpu
from jax.sharding import PartitionSpec as P

MESH = pl.DeviceIdType.MESH
F32 = jnp.float32
BF16 = jnp.bfloat16
CHUNKS = 8
GROUPS = 1
OUTS = 2
NN = (((1,), (0,)), ((), ()))


def split(value):
    high = value.astype(BF16)
    return high, (value - high.astype(F32)).astype(BF16)


def product(left, right, dims=NN):
    dot = functools.partial(lax.dot_general, dimension_numbers=dims, preferred_element_type=F32)
    (lh, ll), (rh, rl) = left, right
    return dot(lh, rh) + (dot(lh, rl) + dot(ll, rh))


def left_form(real, imag):
    return jnp.concatenate(
        [jnp.concatenate([real, -imag], 1), jnp.concatenate([imag, real], 1)], 0
    )


def dagger_form(real, imag):
    real, imag = real.T, imag.T
    return jnp.concatenate(
        [jnp.concatenate([real, -imag], 1), jnp.concatenate([imag, real], 1)], 0
    )


def kernel(
    retain_hbm, hop_hbm, src_hbm, scr_hbm, g, out_se,
    retain, hop, src, scr, lefts, rights, bases, stage, entering, landed, own_map, early,
    load_sem, chain_send, chain_recv, swap_send, swap_recv, early_send, early_recv,
):
    slabs, _, size, _ = hop.shape
    energies, rows = stage.shape[1], stage.shape[3]
    space, energy = lax.axis_index("space"), lax.axis_index("energy")
    stages = lax.axis_size("space")
    piece = size // CHUNKS
    relays = (space % 2 == 0) & (space > 0) & (space < stages - 1)
    paired = (space % 2 == 1) & (space > 1)

    loads = [
        pltpu.make_async_copy(hop_hbm.at[:, 0], hop, load_sem.at[0]),
        pltpu.make_async_copy(src_hbm.at[:, 0], src, load_sem.at[1]),
        pltpu.make_async_copy(scr_hbm, scr, load_sem.at[2]),
        pltpu.make_async_copy(retain_hbm, retain, load_sem.at[3]),
    ]
    for load in loads:
        load.start()

    barrier = pltpu.get_barrier_semaphore()
    for step in range(1, energies):
        pl.semaphore_signal(
            barrier, inc=1, device_id=(space, lax.rem(energy + step, energies)), device_id_type=MESH
        )

    @pl.when(space > 0)
    def _():
        pl.semaphore_signal(barrier, inc=1, device_id=(space - 1, energy), device_id_type=MESH)

    loads[3].wait()
    loads[0].wait()
    loads[1].wait()

    eye = (
        lax.broadcasted_iota(jnp.int32, (size, size), 0)
        == lax.broadcasted_iota(jnp.int32, (size, size), 1)
    ).astype(F32)
    couplers = []
    for j in range(slabs):
        factor = retain[j]
        couplers.append((factor * (eye + hop[j, 0]), factor * hop[j, 1]))

    def sandwich(left, right, real, imag):
        turned = product(split(jnp.concatenate([real, imag], 1)), right)
        return product(left, split(jnp.concatenate([turned[:, :size], turned[:, size:]], 0)))

    base = jnp.concatenate([src[0, 0], src[0, 1]], 0)
    bases[0] = base
    step_lefts = [None]
    for j in range(1, slabs):
        step_left = split(left_form(*couplers[j]))
        step_right = split(dagger_form(*couplers[j]))
        step_lefts.append(step_left)
        base = sandwich(step_left, step_right, base[:size], base[size:]) + jnp.concatenate(
            [src[j, 0], src[j, 1]], 0
        )
        bases[j] = base

    def chain(c, relay=False):
        part = pl.ds(c * piece, piece)
        return pltpu.make_async_remote_copy(
            src_ref=entering.at[:, part] if relay else g.at[slabs - 1, :, part],
            dst_ref=entering.at[:, part],
            send_sem=chain_send.at[c],
            recv_sem=chain_recv.at[c],
            device_id=(space + 1, energy),
            device_id_type=MESH,
        )

    def ahead(i):
        return pltpu.make_async_remote_copy(
            src_ref=bases.at[slabs - 1] if i else own_map,
            dst_ref=early.at[i],
            send_sem=early_send.at[i],
            recv_sem=early_recv.at[i],
            device_id=(space + 1, energy),
            device_id_type=MESH,
        )

    def swap(j, step):
        peer = lax.rem(energy + step, energies)
        return pltpu.make_async_remote_copy(
            src_ref=stage.at[j, peer],
            dst_ref=landed.at[j, energy],
            send_sem=swap_send.at[j, step],
            recv_sem=swap_recv.at[j, step],
            device_id=(space, peer),
            device_id_type=MESH,
        )

    def keep(j, real, imag):
        for ref, form in ((lefts, left_form), (rights, dagger_form)):
            high, low = split(form(real, imag))
            ref[j, 0] = high
            ref[j, 1] = low

    def put(j, block):
        g[j, 0] = block[:size]
        g[j, 1] = block[size:]

    def spread(j):
        for q in range(energies):
            for part in range(2):
                stage[j, q, part] = g[j, part, q * rows : (q + 1) * rows]
        for step in range(1, energies):
            swap(j, step).start()

    pl.semaphore_wait(barrier, energies - 1 + (space < stages - 1).astype(jnp.int32))

    last = slabs - 1

    @pl.when(space == 0)
    def _():
        put(last, bases[last])

        @pl.when(space < stages - 1)
        def _():
            for c in range(CHUNKS):
                chain(c).start()

        spread(last)
        for j in range(last - 1, -1, -1):
            put(j, bases[j])
            spread(j)

    @pl.when(space > 0)
    def _():
        real, imag = couplers[0]
        for j in range(slabs):
            if j > 0:
                both = product(step_lefts[j], split(jnp.concatenate([real, imag], 0)))
                real, imag = both[:size], both[size:]
            keep(j, real, imag)
        own_map[...] = jnp.concatenate([real, imag], 0)

        @pl.when(relays)
        def _():
            ahead(0).start()
            ahead(1).start()

        @pl.when(paired)
        def _():
            ahead(0).wait_recv()
            ahead(1).wait_recv()
            before = split(early[0])
            for j in range(slabs):
                left = lefts[j, 0], lefts[j, 1]
                right = rights[j, 0], rights[j, 1]
                bases[j] = sandwich(left, right, early[1, :size], early[1, size:]) + bases[j]
                both = product(left, before)
                keep(j, both[:size], both[size:])

        turned = []
        for c in range(CHUNKS):
            chain(c).wait_recv()

            @pl.when(relays)
            def _():
                chain(c, True).start()

            if (c + 1) % (CHUNKS // GROUPS) == 0:
                lines = slice((c + 1) * piece - size // GROUPS, (c + 1) * piece)
                arrived = split(jnp.concatenate([entering[0, lines], entering[1, lines]], 1))
                turned.append(product(arrived, (rights[last, 0], rights[last, 1])))
        turned = jnp.concatenate(turned, 0)
        inner = split(jnp.concatenate([turned[:, :size], turned[:, size:]], 0))
        height = size // OUTS
        for o in range(OUTS):
            for part in range(2):
                lines = slice(part * size + o * height, part * size + (o + 1) * height)
                left = lefts[last, 0, lines], lefts[last, 1, lines]
                g[last, part, o * height : (o + 1) * height] = (
                    product(left, inner) + bases[last, lines]
                )

            @pl.when((space < stages - 1) & (space % 2 == 1))
            def _():
                for c in range(o * CHUNKS // OUTS, (o + 1) * CHUNKS // OUTS):
                    chain(c).start()

        spread(last)
        for j in range(last - 1, -1, -1):
            put(
                j,
                sandwich(
                    (lefts[j, 0], lefts[j, 1]),
                    (rights[j, 0], rights[j, 1]),
                    entering[0],
                    entering[1],
                )
                + bases[j],
            )
            spread(j)

    def lanes(part):
        return pl.ds(part, rows, stride=2)

    loads[2].wait()
    for j in range(last, -1, -1):
        landed[j, energy] = stage[j, energy]
        for step in range(1, energies):
            swap(j, step).wait_recv()
        for e in range(energies):
            real = jnp.zeros((rows, size), F32)
            imag = jnp.zeros((rows, size), F32)
            for w in range(e + 1):
                gr, gi = landed[j, e - w, 0], landed[j, e - w, 1]
                sr, si = scr[j, w, lanes(0)], scr[j, w, lanes(1)]
                real = real + (gr * sr - gi * si)
                imag = imag + (gr * si + gi * sr)
            out_se[j, e, lanes(0)] = real
            out_se[j, e, lanes(1)] = imag

    for j in range(slabs):
        for step in range(1, energies):
            swap(j, step).wait_send()

    @pl.when((space < stages - 1) & jnp.logical_not(relays))
    def _():
        for c in range(CHUNKS):
            chain(c).wait_send()

    @pl.when(relays)
    def _():
        ahead(0).wait_send()
        ahead(1).wait_send()
        for c in range(CHUNKS):
            chain(c, True).wait_send()


def write_out(g, se, out_g, out_se, sems):
    copies = [
        pltpu.make_async_copy(g, out_g.at[:, 0], sems.at[0]),
        pltpu.make_async_copy(se, out_se, sems.at[1]),
    ]
    for copy in copies:
        copy.start()
    for copy in copies:
        copy.wait()


def body(retain, hopping, source, screened):
    slabs, _, _, size, _ = hopping.shape
    energies = screened.shape[1]
    rows = screened.shape[3] // size
    woven = (
        screened.reshape(slabs, energies, 2, rows, size)
        .transpose(0, 1, 3, 2, 4)
        .reshape(slabs, energies, 2 * rows, size)
    )
    any_spec = pl.BlockSpec(memory_space=pl.ANY)
    vmem_spec = pl.BlockSpec(memory_space=pltpu.VMEM)
    vmem = pltpu.VMEM
    greens, self_energy = pl.pallas_call(
        kernel,
        out_shape=(vmem((slabs, 2, size, size), F32), vmem(woven.shape, F32)),
        in_specs=[pl.BlockSpec(memory_space=pltpu.HBM)] * 4,
        out_specs=(vmem_spec, vmem_spec),
        scratch_shapes=[
            pltpu.SMEM((slabs,), F32),
            vmem((slabs, 2, size, size), F32),
            vmem((slabs, 2, size, size), F32),
            vmem(woven.shape, F32),
            vmem((slabs, 2, 2 * size, 2 * size), BF16),
            vmem((slabs, 2, 2 * size, 2 * size), BF16),
            vmem((slabs, 2 * size, size), F32),
            vmem((slabs, energies, 2, rows, size), F32),
            vmem((2, size, size), F32),
            vmem((slabs, energies, 2, rows, size), F32),
            vmem((2 * size, size), F32),
            vmem((2, 2 * size, size), F32),
            pltpu.SemaphoreType.DMA((4,)),
            pltpu.SemaphoreType.DMA((CHUNKS,)),
            pltpu.SemaphoreType.DMA((CHUNKS,)),
            pltpu.SemaphoreType.DMA((slabs, energies)),
            pltpu.SemaphoreType.DMA((slabs, energies)),
            pltpu.SemaphoreType.DMA((2,)),
            pltpu.SemaphoreType.DMA((2,)),
        ],
        compiler_params=pltpu.CompilerParams(
            collective_id=0, has_side_effects=True
        ),
    )(retain.reshape(slabs), hopping, source, woven)
    greens, self_energy = pl.pallas_call(
        write_out,
        out_shape=(
            jax.ShapeDtypeStruct(source.shape, F32),
            jax.ShapeDtypeStruct(woven.shape, F32),
        ),
        in_specs=[vmem_spec, vmem_spec],
        out_specs=(any_spec, any_spec),
        scratch_shapes=[pltpu.SemaphoreType.DMA((2,))],
        compiler_params=pltpu.CompilerParams(vmem_limit_bytes=4 << 20),
    )(greens, self_energy)
    return greens, (
        self_energy.reshape(slabs, energies, rows, 2, size)
        .transpose(0, 1, 3, 2, 4)
        .reshape(screened.shape)
    )


def solution(mesh):
    placed = (
        P("space", "energy"),
        P("space", "energy", None, None, None),
        P("space", "energy", None, None, None),
        P("space", None, None, "energy"),
    )
    return jax.shard_map(
        body,
        mesh=mesh,
        in_specs=placed,
        out_specs=(P("space", "energy", None, None, None), P("space", None, None, "energy")),
        check_vma=False,
    )
```

profile of v0, /device:TPU:25, one launch (start us, length us, event | category | flops | bytes accessed | tf_op | source)
XLA Modules:
  0.0 19.5 jit_solution(7734565568223205826)
XLA Ops:
  0.6 18.1 %shard_map.59 = (f32[2,2,128,128]{3,2,1,0:T(8,128)S(1)}, f32[2,8,32,128]{3,2,1,0:T(8,128)S(1)}) custom-call(f32[2]{0:T(128)} %bitcast.12, f32[2,1,2,128,128]{4,3,2,1,0:T(8,128)} %hop_hbm.1, f32[2,1,2,128,128]{4,3,2,1,0:T(8,128)} %src_hbm.1, f32[2,8,32,128]{3,2,1,0:T(8,128)} %bitcast.11), custom_call_target="tpu_custom_call" | custom-call | tf_op jit(solution)/shard_map/pallas_call | solution.py:299
  18.7 0.8 %shard_map.60 = (f32[2,1,2,128,128]{4,3,2,1,0:T(8,128)}, f32[2,8,32,128]{3,2,1,0:T(8,128)}) custom-call(f32[2,2,128,128]{3,2,1,0:T(8,128)S(1)} %get-tuple-element.6.g, f32[2,8,32,128]{3,2,1,0:T(8,128)S(1)} %get-tuple-element.7.se), custom_call_target="tpu_custom_call" | custom-call | tf_op jit(solution)/shard_map/pallas_call | solution.py:329
where the time goes:
time: 19.7 us; the launch traced here: 19.5 us
  Pallas kernels  18.9 us (96%)
  between operations  0.64 us (3%)
    pallas_call x1, Pallas kernels, body(): pl.pallas_call(kernel, out_shape=(vmem((slabs, 2, size, size), F32), vmem...  18.1 us
    pallas_call x1, Pallas kernels, body(): pl.pallas_call(write_out, out_shape=(jax.ShapeDtypeStruct(source.shape, F...  0.81 us

commit v1 on v0

--- a/solution.py
+++ b/solution.py
@@ -11,8 +11,10 @@
 F32 = jnp.float32
 BF16 = jnp.bfloat16
 CHUNKS = 8
-GROUPS = 1
+GROUPS = 4
 OUTS = 2
+LEAD = 1
+ORDER = {6: 0, 4: 1, 7: 2, 5: 3, 2: 4, 3: 5, 1: 1 << 30}
 NN = (((1,), (0,)), ((), ()))
 
 
@@ -42,22 +44,31 @@
 
 def kernel(
     retain_hbm, hop_hbm, src_hbm, scr_hbm, g, out_se,
-    retain, hop, src, scr, lefts, rights, bases, stage, entering, landed, own_map, early,
-    load_sem, chain_send, chain_recv, swap_send, swap_recv, early_send, early_recv,
+    retain, slabs_in, scr, lefts, rights, bases, entering, landed, own, early,
+    load_sem, chain_send, chain_recv, swap_send, swap_recv, ahead_sem, turn,
 ):
-    slabs, _, size, _ = hop.shape
-    energies, rows = stage.shape[1], stage.shape[3]
+    _, slabs, _, size, _ = slabs_in.shape
+    energies, rows = landed.shape[1], landed.shape[3]
     space, energy = lax.axis_index("space"), lax.axis_index("energy")
     stages = lax.axis_size("space")
     piece = size // CHUNKS
-    relays = (space % 2 == 0) & (space > 0) & (space < stages - 1)
-    paired = (space % 2 == 1) & (space > 1)
+    last = slabs - 1
+    even = energies % 2 == 0
+    power = energies & (energies - 1) == 0
+    partner = energy + 1 - 2 * lax.rem(energy, 2)
+    second = lax.rem(energy, 2) == 0
+    middle = (space > 0) & (space < stages - 1)
+    odd = lax.rem(space, 2) == 1
+    leaps = second & odd & (space < stages - 2)
+    gives = second & middle & jnp.logical_not(odd)
+    takes = second & odd & (space > 1)
+    hop, src = slabs_in.at[0], slabs_in.at[1]
 
     loads = [
         pltpu.make_async_copy(hop_hbm.at[:, 0], hop, load_sem.at[0]),
-        pltpu.make_async_copy(src_hbm.at[:, 0], src, load_sem.at[1]),
-        pltpu.make_async_copy(scr_hbm, scr, load_sem.at[2]),
-        pltpu.make_async_copy(retain_hbm, retain, load_sem.at[3]),
+        pltpu.make_async_copy(src_hbm.at[:, 0], src, load_sem.at[0]),
+        pltpu.make_async_copy(scr_hbm, scr, load_sem.at[1]),
+        pltpu.make_async_copy(retain_hbm, retain, load_sem.at[2]),
     ]
     for load in loads:
         load.start()
@@ -72,9 +83,12 @@
     def _():
         pl.semaphore_signal(barrier, inc=1, device_id=(space - 1, energy), device_id_type=MESH)
 
+    @pl.when(takes)
+    def _():
+        pl.semaphore_signal(barrier, inc=1, device_id=(space - 2, energy), device_id_type=MESH)
+
     loads[3].wait()
-    loads[0].wait()
-    loads[1].wait()
+    pltpu.make_async_copy(slabs_in, slabs_in, load_sem.at[0]).wait()
 
     eye = (
         lax.broadcasted_iota(jnp.int32, (size, size), 0)
@@ -101,34 +115,51 @@
         )
         bases[j] = base
 
-    def chain(c, relay=False):
-        part = pl.ds(c * piece, piece)
+    def chain(lines, reach, sem):
         return pltpu.make_async_remote_copy(
-            src_ref=entering.at[:, part] if relay else g.at[slabs - 1, :, part],
-            dst_ref=entering.at[:, part],
-            send_sem=chain_send.at[c],
-            recv_sem=chain_recv.at[c],
+            src_ref=g.at[last, :, lines],
+            dst_ref=entering.at[:, lines],
+            send_sem=chain_send.at[sem],
+            recv_sem=chain_recv.at[lines.start // (size // GROUPS)],
+            device_id=(space + reach, energy),
+            device_id_type=MESH,
+        )
+
+    def send_on(first, count, reach=1):
+        for c in range(first, first + count):
+            chain(pl.ds(c * piece, piece), reach, int(c == LEAD)).start()
+
+    def sent(times):
+        for _ in range(times):
+            chain(pl.ds(0, piece), 1, 1).wait_send()
+            chain(pl.ds(0, size - piece), 1, 0).wait_send()
+
+    def ahead(i):
+        return pltpu.make_async_remote_copy(
+            src_ref=own.at[i],
+            dst_ref=early.at[i],
+            send_sem=ahead_sem.at[0],
+            recv_sem=ahead_sem.at[1],
             device_id=(space + 1, energy),
             device_id_type=MESH,
         )
 
-    def ahead(i):
+    def aheads():
         return pltpu.make_async_remote_copy(
-            src_ref=bases.at[slabs - 1] if i else own_map,
-            dst_ref=early.at[i],
-            send_sem=early_send.at[i],
-            recv_sem=early_recv.at[i],
+            src_ref=own,
+            dst_ref=early,
+            send_sem=ahead_sem.at[0],
+            recv_sem=ahead_sem.at[1],
             device_id=(space + 1, energy),
             device_id_type=MESH,
         )
 
-    def swap(j, step):
-        peer = lax.rem(energy + step, energies)
+    def swap(j, peer):
         return pltpu.make_async_remote_copy(
-            src_ref=stage.at[j, peer],
+            src_ref=g.at[j, :, pl.ds(pl.multiple_of(peer * rows, rows), rows)],
             dst_ref=landed.at[j, energy],
-            send_sem=swap_send.at[j, step],
-            recv_sem=swap_recv.at[j, step],
+            send_sem=swap_send.at[0],
+            recv_sem=swap_recv.at[j],
             device_id=(space, peer),
             device_id_type=MESH,
         )
@@ -144,29 +175,9 @@
         g[j, 1] = block[size:]
 
     def spread(j):
-        for q in range(energies):
-            for part in range(2):
-                stage[j, q, part] = g[j, part, q * rows : (q + 1) * rows]
-        for step in range(1, energies):
-            swap(j, step).start()
-
-    pl.semaphore_wait(barrier, energies - 1 + (space < stages - 1).astype(jnp.int32))
-
-    last = slabs - 1
-
-    @pl.when(space == 0)
-    def _():
-        put(last, bases[last])
-
-        @pl.when(space < stages - 1)
-        def _():
-            for c in range(CHUNKS):
-                chain(c).start()
-
-        spread(last)
-        for j in range(last - 1, -1, -1):
-            put(j, bases[j])
-            spread(j)
+        order = sorted(range(1, energies), key=lambda k: ORDER.get(k, k))
+        for k in order:
+            swap(j, jnp.bitwise_xor(energy, k) if power else lax.rem(energy + k, energies)).start()
 
     @pl.when(space > 0)
     def _():
@@ -176,17 +187,57 @@
                 both = product(step_lefts[j], split(jnp.concatenate([real, imag], 0)))
                 real, imag = both[:size], both[size:]
             keep(j, real, imag)
-        own_map[...] = jnp.concatenate([real, imag], 0)
-
-        @pl.when(relays)
+
+        @pl.when(gives)
+        def _():
+            own[0] = jnp.concatenate([real, imag], 0)
+            own[1] = bases[last]
+
+    pl.semaphore_wait(
+        barrier,
+        energies - 1 + (space < stages - 1).astype(jnp.int32) + leaps.astype(jnp.int32),
+    )
+
+    def give_turn():
+        pl.semaphore_signal(turn, inc=1, device_id=(space, partner), device_id_type=MESH)
+
+    @pl.when(space == 0)
+    def _():
+        put(last, bases[last])
+        if stages > 1 and even:
+            @pl.when(second)
+            def _():
+                pl.semaphore_wait(turn, 1)
+                send_on(0, CHUNKS)
+                give_turn()
+
+            @pl.when(jnp.logical_not(second))
+            def _():
+                send_on(0, CHUNKS)
+                chain(pl.ds(0, piece), 1, 1).wait_send()
+                give_turn()
+        elif stages > 1:
+            send_on(0, CHUNKS)
+
+        for j in range(last - 1, -1, -1):
+            put(j, bases[j])
+        if stages > 1 and even:
+            @pl.when(jnp.logical_not(second))
+            def _():
+                pl.semaphore_wait(turn, 1)
+        for j in range(last, -1, -1):
+            spread(j)
+
+    @pl.when(space > 0)
+    def _():
+        @pl.when(gives)
         def _():
             ahead(0).start()
             ahead(1).start()
 
-        @pl.when(paired)
-        def _():
-            ahead(0).wait_recv()
-            ahead(1).wait_recv()
+        @pl.when(takes)
+        def _():
+            aheads().wait_recv()
             before = split(early[0])
             for j in range(slabs):
                 left = lefts[j, 0], lefts[j, 1]
@@ -196,17 +247,11 @@
                 keep(j, both[:size], both[size:])
 
         turned = []
-        for c in range(CHUNKS):
-            chain(c).wait_recv()
-
-            @pl.when(relays)
-            def _():
-                chain(c, True).start()
-
-            if (c + 1) % (CHUNKS // GROUPS) == 0:
-                lines = slice((c + 1) * piece - size // GROUPS, (c + 1) * piece)
-                arrived = split(jnp.concatenate([entering[0, lines], entering[1, lines]], 1))
-                turned.append(product(arrived, (rights[last, 0], rights[last, 1])))
+        for c in range(GROUPS):
+            lines = pl.ds(c * (size // GROUPS), size // GROUPS)
+            chain(lines, 1, 0).wait_recv()
+            arrived = split(jnp.concatenate([entering[0, lines], entering[1, lines]], 1))
+            turned.append(product(arrived, (rights[last, 0], rights[last, 1])))
         turned = jnp.concatenate(turned, 0)
         inner = split(jnp.concatenate([turned[:, :size], turned[:, size:]], 0))
         height = size // OUTS
@@ -218,33 +263,51 @@
                     product(left, inner) + bases[last, lines]
                 )
 
-            @pl.when((space < stages - 1) & (space % 2 == 1))
-            def _():
-                for c in range(o * CHUNKS // OUTS, (o + 1) * CHUNKS // OUTS):
-                    chain(c).start()
-
+            @pl.when(middle & jnp.logical_not(second))
+            def _():
+                send_on(o * CHUNKS // OUTS, CHUNKS // OUTS)
+
+            @pl.when(leaps)
+            def _():
+                send_on(o * CHUNKS // OUTS, CHUNKS // OUTS, 2)
+
+        @pl.when(second & odd & middle)
+        def _():
+            send_on(0, CHUNKS)
+            if even:
+                give_turn()
+
+        def rest():
+            for j in range(last - 1, -1, -1):
+                put(
+                    j,
+                    sandwich(
+                        (lefts[j, 0], lefts[j, 1]),
+                        (rights[j, 0], rights[j, 1]),
+                        entering[0],
+                        entering[1],
+                    )
+                    + bases[j],
+                )
+
+        if even:
+            @pl.when(jnp.logical_not(second) & odd & middle)
+            def _():
+                pl.semaphore_wait(turn, 1)
         spread(last)
+        rest()
         for j in range(last - 1, -1, -1):
-            put(
-                j,
-                sandwich(
-                    (lefts[j, 0], lefts[j, 1]),
-                    (rights[j, 0], rights[j, 1]),
-                    entering[0],
-                    entering[1],
-                )
-                + bases[j],
-            )
             spread(j)
 
     def lanes(part):
         return pl.ds(part, rows, stride=2)
 
     loads[2].wait()
+    mine = pl.ds(pl.multiple_of(energy * rows, rows), rows)
     for j in range(last, -1, -1):
-        landed[j, energy] = stage[j, energy]
-        for step in range(1, energies):
-            swap(j, step).wait_recv()
+        landed[j, energy] = g[j, :, mine]
+        others = landed.at[j, pl.ds(0, energies - 1)]
+        pltpu.make_async_copy(others, others, swap_recv.at[j]).wait()
         for e in range(energies):
             real = jnp.zeros((rows, size), F32)
             imag = jnp.zeros((rows, size), F32)
@@ -256,21 +319,29 @@
             out_se[j, e, lanes(0)] = real
             out_se[j, e, lanes(1)] = imag
 
-    for j in range(slabs):
-        for step in range(1, energies):
-            swap(j, step).wait_send()
-
-    @pl.when((space < stages - 1) & jnp.logical_not(relays))
-    def _():
-        for c in range(CHUNKS):
-            chain(c).wait_send()
-
-    @pl.when(relays)
-    def _():
-        ahead(0).wait_send()
-        ahead(1).wait_send()
-        for c in range(CHUNKS):
-            chain(c, True).wait_send()
+    others = landed.at[:, pl.ds(0, energies - 1)]
+    pltpu.make_async_copy(others, others, swap_send.at[0]).wait()
+
+    @pl.when(gives)
+    def _():
+        aheads().wait_send()
+
+    if even:
+        @pl.when((space == 0) & jnp.logical_not(second) & (stages > 1))
+        def _():
+            chain(pl.ds(0, size - piece), 1, 0).wait_send()
+
+        @pl.when(((space == 0) & second & (stages > 1)) | (middle & (jnp.logical_not(second) | odd)))
+        def _():
+            sent(1)
+    else:
+        @pl.when((space == 0) & (stages > 1) | (middle & (jnp.logical_not(second) | odd)))
+        def _():
+            sent(1)
+
+    @pl.when(leaps)
+    def _():
+        sent(1)
 
 
 def write_out(g, se, out_g, out_se, sems):
@@ -303,24 +374,22 @@
         out_specs=(vmem_spec, vmem_spec),
         scratch_shapes=[
             pltpu.SMEM((slabs,), F32),
-            vmem((slabs, 2, size, size), F32),
-            vmem((slabs, 2, size, size), F32),
+            vmem((2, slabs, 2, size, size), F32),
             vmem(woven.shape, F32),
             vmem((slabs, 2, 2 * size, 2 * size), BF16),
             vmem((slabs, 2, 2 * size, 2 * size), BF16),
             vmem((slabs, 2 * size, size), F32),
-            vmem((slabs, energies, 2, rows, size), F32),
             vmem((2, size, size), F32),
             vmem((slabs, energies, 2, rows, size), F32),
-            vmem((2 * size, size), F32),
             vmem((2, 2 * size, size), F32),
-            pltpu.SemaphoreType.DMA((4,)),
-            pltpu.SemaphoreType.DMA((CHUNKS,)),
-            pltpu.SemaphoreType.DMA((CHUNKS,)),
-            pltpu.SemaphoreType.DMA((slabs, energies)),
-            pltpu.SemaphoreType.DMA((slabs, energies)),
+            vmem((2, 2 * size, size), F32),
+            pltpu.SemaphoreType.DMA((3,)),
             pltpu.SemaphoreType.DMA((2,)),
+            pltpu.SemaphoreType.DMA((GROUPS,)),
+            pltpu.SemaphoreType.DMA((1,)),
+            pltpu.SemaphoreType.DMA((slabs,)),
             pltpu.SemaphoreType.DMA((2,)),
+            pltpu.SemaphoreType.REGULAR,
         ],
         compiler_params=pltpu.CompilerParams(
             collective_id=0, has_side_effects=True

time: 19.7 us -> 18.8 us (0.954)
  the two profiles are of different devices: /device:TPU:25 before, /device:TPU:17 now
where the time goes in v1:
time: 18.8 us; the launch traced here: 18.6 us
  Pallas kernels  18 us (96%)
  between operations  0.64 us (3%)
    pallas_call x1, Pallas kernels, body(): pl.pallas_call(kernel, out_shape=(vmem((slabs, 2, size, size), F32), vmem...  17.2 us
    pallas_call x1, Pallas kernels, body(): pl.pallas_call(write_out, out_shape=(jax.ShapeDtypeStruct(source.shape, F...  0.81 us

profile of v1, /device:TPU:17, one launch (start us, length us, event | category | flops | bytes accessed | tf_op | source)
XLA Modules:
  0.0 18.6 jit_solution(12406082574139459622)
XLA Ops:
  0.6 17.2 %shard_map.59 = (f32[2,2,128,128]{3,2,1,0:T(8,128)S(1)}, f32[2,8,32,128]{3,2,1,0:T(8,128)S(1)}) custom-call(f32[2]{0:T(128)} %bitcast.12, f32[2,1,2,128,128]{4,3,2,1,0:T(8,128)} %hop_hbm.1, f32[2,1,2,128,128]{4,3,2,1,0:T(8,128)} %src_hbm.1, f32[2,8,32,128]{3,2,1,0:T(8,128)} %bitcast.11), custom_call_target="tpu_custom_call" | custom-call | tf_op jit(solution)/shard_map/pallas_call | solution.py:370
  17.8 0.8 %shard_map.60 = (f32[2,1,2,128,128]{4,3,2,1,0:T(8,128)}, f32[2,8,32,128]{3,2,1,0:T(8,128)}) custom-call(f32[2,2,128,128]{3,2,1,0:T(8,128)S(1)} %get-tuple-element.6.g, f32[2,8,32,128]{3,2,1,0:T(8,128)S(1)} %get-tuple-element.7.se), custom_call_target="tpu_custom_call" | custom-call | tf_op jit(solution)/shard_map/pallas_call | solution.py:398

commit v2 on v1

v2 whole, which is shorter than its diff:
```python
import functools

import jax
import jax.numpy as jnp
from jax import lax
from jax.experimental import pallas as pl
from jax.experimental.pallas import tpu as pltpu
from jax.sharding import PartitionSpec as P

MESH = pl.DeviceIdType.MESH
F32 = jnp.float32
BF16 = jnp.bfloat16
CHUNKS = 8
GROUPS = 4
OUTS = 2
ORDER = {6: 0, 4: 1, 7: 2, 5: 3, 2: 4, 3: 5, 1: 1 << 30}


def split(value):
    high = value.astype(BF16)
    return high, (value - high.astype(F32)).astype(BF16)


dot = functools.partial(
    lax.dot_general, dimension_numbers=(((1,), (0,)), ((), ())), preferred_element_type=F32
)


def rows_by(block, right):
    (high, low), (rh, rl) = split(block), right
    count = high.shape[0]
    both = dot(jnp.concatenate([high, low], 0), rh)
    return both[:count] + (dot(high, rl) + both[count:])


def left_form(real, imag):
    return jnp.concatenate(
        [jnp.concatenate([real, -imag], 1), jnp.concatenate([imag, real], 1)], 0
    )


def dagger_form(real, imag):
    real, imag = real.T, imag.T
    return jnp.concatenate(
        [jnp.concatenate([real, -imag], 1), jnp.concatenate([imag, real], 1)], 0
    )


def arranged(form):
    size = form.shape[0] // 2
    height = size // OUTS
    high, low = split(form)
    return [
        jnp.concatenate(
            [x[p * size + o * height : p * size + (o + 1) * height] for x in (high, low) for p in range(2)], 0
        )
        for o in range(OUTS)
    ]


def part_by(left, right):
    height, size = left.shape[0] // 4, right.shape[1] // 2
    product = dot(left, right)
    cross = product[: 2 * height, size:] + product[2 * height :, :size]
    both = product[: 2 * height, :size] + cross
    return both[:height], both[height:]


def columns_by(left, block):
    right = stacked(block)
    parts = [part_by(x, right) for x in left]
    return jnp.concatenate([p[0] for p in parts] + [p[1] for p in parts], 0)


def stacked(block):
    return jnp.concatenate(split(block), 1)


def turned_block(turned):
    size = turned.shape[1] // 2
    return jnp.concatenate([turned[:, :size], turned[:, size:]], 0)


def kernel(
    retain_hbm, hop_hbm, src_hbm, scr_hbm, g, out_se,
    retain, slabs_in, scr, lefts, rights, bases, entering, landed, own, early, guest, passed, spun,
    load_sem, chain_send, chain_recv, guest_recv, swap_send, swap_recv, ahead_sem, turn,
):
    _, slabs, _, size, _ = slabs_in.shape
    energies, rows = landed.shape[1], landed.shape[3]
    space, energy = lax.axis_index("space"), lax.axis_index("energy")
    stages = lax.axis_size("space")
    piece, height, group = size // CHUNKS, size // OUTS, size // GROUPS
    last = slabs - 1
    paired = energies % 2 == 0
    power = energies & (energies - 1) == 0 and energies >= OUTS
    order = sorted(range(1, energies), key=lambda k: ORDER.get(k, k))
    hop, src = slabs_in.at[0], slabs_in.at[1]

    odd = lax.rem(space, 2) == 1
    middle = (space > 0) & (space < stages - 1)
    if paired:
        partner = energy + 1 - 2 * lax.rem(energy, 2)
        second = lax.rem(energy, 2) == 0
    else:
        partner = energy
        second = energy < 0
    first = jnp.logical_not(second)
    hosts = first & odd & middle & paired
    hosted = second & odd & middle
    gives = second & middle & jnp.logical_not(odd)
    takes = second & odd & (space > 1)
    leaps = hosts & (space + 2 < stages)
    carries = (first & (space < stages - 1)) | (second & (space == 0) & (stages > 1))
    stops = (space == stages - 1) | gives

    loads = [
        pltpu.make_async_copy(retain_hbm, retain, load_sem.at[2]),
        pltpu.make_async_copy(hop_hbm.at[:, 0], hop, load_sem.at[0]),
        pltpu.make_async_copy(src_hbm.at[:, 0], src, load_sem.at[0]),
        pltpu.make_async_copy(scr_hbm, scr, load_sem.at[1]),
    ]
    for load in loads:
        load.start()

    barrier = pltpu.get_barrier_semaphore()

    def greet(where, who):
        pl.semaphore_signal(barrier, inc=1, device_id=(where, who), device_id_type=MESH)

    for step in range(1, energies):
        greet(space, lax.rem(energy + step, energies))

    @pl.when((first & (space > 0)) | takes)
    def _():
        greet(space - 1, energy)

    if paired:
        @pl.when(((space == 1) & hosts) | (second & (space > 0) & jnp.logical_not(odd)))
        def _():
            greet(space - 1, partner)

        @pl.when((space == 1) & second & (stages == 2))
        def _():
            greet(space - 1, energy)

        @pl.when(hosts & (space > 1))
        def _():
            greet(space - 2, energy)

        @pl.when(takes & (space == stages - 1))
        def _():
            greet(space - 2, partner)

    greeted = (
        energies - 1
        + carries.astype(jnp.int32)
        + hosts.astype(jnp.int32)
        + leaps.astype(jnp.int32)
        + gives.astype(jnp.int32)
    )

    def enter():
        pl.semaphore_wait(barrier, greeted)

    loads[0].wait()
    pltpu.make_async_copy(slabs_in, slabs_in, load_sem.at[0]).wait()

    eye = (
        lax.broadcasted_iota(jnp.int32, (size, size), 0)
        == lax.broadcasted_iota(jnp.int32, (size, size), 1)
    ).astype(F32)
    couplers = []
    for j in range(slabs):
        factor = retain[j]
        couplers.append((factor * (eye + hop[j, 0]), factor * hop[j, 1]))

    def sandwich(left, right, block):
        wide = jnp.concatenate([block[:size], block[size:]], 1)
        return columns_by(left, turned_block(rows_by(wide, right)))

    def source(j):
        return jnp.concatenate([src[j, 0], src[j, 1]], 0)

    step_lefts, step_rights = [None], [None]
    for j in range(1, slabs):
        step_lefts.append(arranged(left_form(*couplers[j])))
        step_rights.append(split(dagger_form(*couplers[j])))

    def copy(source_ref, target_ref, sems, where, who, wait=0):
        return pltpu.make_async_remote_copy(
            src_ref=source_ref,
            dst_ref=target_ref,
            send_sem=sems[0],
            recv_sem=sems[1],
            device_id=(where, who),
            device_id_type=MESH,
        )

    def line(source_ref, target_ref, recv, start, count, where, who, sem=0):
        lines = pl.ds(start, count)
        return copy(
            source_ref.at[:, lines],
            target_ref.at[:, lines],
            (chain_send.at[sem], recv.at[start // group]),
            where,
            who,
        )

    made = g.at[last]

    def send_on(begin, count, to_guest=False):
        for c in range(begin, begin + count):
            if to_guest:
                line(made, guest, guest_recv, c * piece, piece, space + 1, partner).start()
            else:
                line(made, entering, chain_recv, c * piece, piece, space + 1, energy, sem=int(c == 0)).start()

    def sent(count, sem=0):
        line(made, entering, chain_recv, 0, count, space, energy, sem=sem).wait_send()

    def ahead(refs, where, who):
        return copy(refs[0], refs[1], (ahead_sem.at[0], ahead_sem.at[1]), where, who)

    def hand(where, who):
        for i in range(2):
            ahead((own.at[i], early.at[i]), where, who).start()

    def swap(j, peer):
        return copy(
            g.at[j, :, pl.ds(pl.multiple_of(peer * rows, rows), rows)],
            landed.at[j, energy],
            (swap_send.at[0], swap_recv.at[j]),
            space,
            peer,
        )

    def spread(j):
        for k in order:
            swap(j, jnp.bitwise_xor(energy, k) if power else lax.rem(energy + k, energies)).start()

    def part_spread(j, o):
        half = energies // OUTS
        near = [k for k in order if k < half]
        far = [k for k in order if half <= k]
        for ks, there in ((near, energy // half == o), (far, energy // half != o)):
            @pl.when(there)
            def _():
                for k in ks:
                    swap(j, jnp.bitwise_xor(energy, k)).start()

    def keep(j, block):
        real, imag = block[:size], block[size:]
        for o, part in enumerate(arranged(left_form(real, imag))):
            lefts[j, o] = part
        rights[j, 0], rights[j, 1] = split(dagger_form(real, imag))

    def left_of(j):
        return [lefts[j, o] for o in range(OUTS)]

    def right_of(j):
        return rights[j, 0], rights[j, 1]

    def finish(target, o, left, inner, more):
        for part, value in enumerate(part_by(left, inner)):
            target[part, o * height : (o + 1) * height] = value + more(part)

    def base_part(j, o):
        return lambda part: bases[j, part * size + o * height : part * size + (o + 1) * height]

    def give_turn():
        pl.semaphore_signal(turn, inc=1, device_id=(space, partner), device_id_type=MESH)

    @pl.when(space == 0)
    def _():
        base = source(0)
        for j in range(1, slabs):
            g[j - 1, 0] = base[:size]
            g[j - 1, 1] = base[size:]
            if j < last:
                base = sandwich(step_lefts[j], step_rights[j], base) + source(j)
        wide = jnp.concatenate([base[:size], base[size:]], 1)
        inner = stacked(turned_block(rows_by(wide, step_rights[last])))
        for o in range(OUTS):
            finish(
                made,
                o,
                step_lefts[last][o],
                inner,
                lambda part: src[last, part, o * height : (o + 1) * height],
            )
            if o == 0:
                enter()
            if stages > 1:
                @pl.when(first)
                def _():
                    send_on(o * CHUNKS // OUTS, CHUNKS // OUTS)
        if stages > 1 and paired:
            @pl.when(second)
            def _():
                pl.semaphore_wait(turn, 1)
                if stages > 2:
                    send_on(0, CHUNKS, True)
                else:
                    send_on(0, CHUNKS)
                give_turn()

            @pl.when(first)
            def _():
                sent(piece, 1)
                give_turn()
                pl.semaphore_wait(turn, 1)

        for j in range(last, -1, -1):
            spread(j)

    @pl.when(space > 0)
    def _():
        base = source(0)
        bases[0] = base
        for j in range(1, slabs):
            base = sandwich(step_lefts[j], step_rights[j], base) + source(j)
            bases[j] = base
        block = jnp.concatenate(couplers[0], 0)
        for j in range(slabs):
            if j > 0:
                block = columns_by(step_lefts[j], block)
            keep(j, block)

        @pl.when(gives | (hosted & (space == 1)))
        def _():
            own[0] = block
            own[1] = bases[last]
        enter()

        @pl.when(gives)
        def _():
            hand(space + 1, energy)

        @pl.when(takes)
        def _():
            ahead((own, early), space, energy).wait_recv()
            for j in range(slabs):
                left = left_of(j)
                bases[j] = sandwich(left, right_of(j), early[1]) + bases[j]
                block = columns_by(left, early[0])
                keep(j, block)
                if j == last:
                    @pl.when(hosted)
                    def _():
                        own[0] = block
                        own[1] = bases[last]

        if paired:
            @pl.when(hosted)
            def _():
                hand(space, partner)

            @pl.when(hosts)
            def _():
                ahead((own, early), space, energy).wait_recv()
                keep(slabs, early[0])

        turned = []
        for c in range(GROUPS):
            line(made, entering, chain_recv, c * group, group, space, energy).wait_recv()
            lines = pl.ds(c * group, group)
            arrived = jnp.concatenate([entering[0, lines], entering[1, lines]], 1)
            turned.append(rows_by(arrived, right_of(last)))
            if c < GROUPS - 1:
                for j in range(last):
                    spun[j, lines] = rows_by(arrived, right_of(j))

        inner = stacked(turned_block(jnp.concatenate(turned, 0)))
        for o in range(OUTS):
            finish(made, o, lefts[last, o], inner, base_part(last, o))

            @pl.when(middle & first)
            def _():
                send_on(o * CHUNKS // OUTS, CHUNKS // OUTS)

            if power:
                @pl.when(stops)
                def _():
                    part_spread(last, o)

        if paired:
            @pl.when(hosts)
            def _():
                turned = []
                for c in range(GROUPS):
                    line(made, guest, guest_recv, c * group, group, space, energy).wait_recv()
                    line(guest, entering, chain_recv, c * group, group, space, partner).start()
                    lines = pl.ds(c * group, group)
                    arrived = jnp.concatenate([guest[0, lines], guest[1, lines]], 1)
                    turned.append(rows_by(arrived, right_of(slabs)))
                inner = stacked(turned_block(jnp.concatenate(turned, 0)))
                for o in range(OUTS):
                    finish(
                        passed,
                        o,
                        lefts[slabs, o],
                        inner,
                        lambda part: early[
                            1, part * size + o * height : part * size + (o + 1) * height
                        ],
                    )
                    chunks = range(o * CHUNKS // OUTS, (o + 1) * CHUNKS // OUTS)

                    @pl.when(leaps & (space + 2 < stages - 1))
                    def _():
                        for c in chunks:
                            line(passed, guest, guest_recv, c * piece, piece, space + 2, energy).start()

                    @pl.when(leaps & (space + 2 == stages - 1))
                    def _():
                        for c in chunks:
                            line(
                                passed, entering, chain_recv, c * piece, piece, space + 2, partner
                            ).start()

                for c in range(CHUNKS):
                    line(passed, entering, chain_recv, c * piece, piece, space + 1, partner).start()
                give_turn()

            @pl.when(hosted)
            def _():
                pl.semaphore_wait(turn, 1)

        @pl.when(jnp.logical_not(stops) if power else True)
        def _():
            spread(last)

        for j in range(last - 1, -1, -1):
            tail = pl.ds(size - group, group)
            spun[j, tail] = rows_by(arrived, right_of(j))
            inner = stacked(turned_block(spun[j]))
            for o in range(OUTS):
                finish(g.at[j], o, lefts[j, o], inner, base_part(j, o))
                if power:
                    part_spread(j, o)
            if not power:
                spread(j)

    def lanes(part):
        return pl.ds(part, rows, stride=2)

    loads[3].wait()
    mine = pl.ds(pl.multiple_of(energy * rows, rows), rows)
    for j in range(last, -1, -1):
        landed[j, energy] = g[j, :, mine]
        others = landed.at[j, pl.ds(0, energies - 1)]
        pltpu.make_async_copy(others, others, swap_recv.at[j]).wait()
        for e in range(energies):
            real = jnp.zeros((rows, size), F32)
            imag = jnp.zeros((rows, size), F32)
            for w in range(e + 1):
                gr, gi = landed[j, e - w, 0], landed[j, e - w, 1]
                sr, si = scr[j, w, lanes(0)], scr[j, w, lanes(1)]
                real = real + (gr * sr - gi * si)
                imag = imag + (gr * si + gi * sr)
            out_se[j, e, lanes(0)] = real
            out_se[j, e, lanes(1)] = imag

    others = landed.at[:, pl.ds(0, energies - 1)]
    pltpu.make_async_copy(others, others, swap_send.at[0]).wait()

    @pl.when(gives | hosted)
    def _():
        ahead((own, early), space, energy).wait_send()

    @pl.when(first & (space < stages - 1))
    def _():
        sent(size - piece)
        if not paired:
            sent(piece, 1)

    if paired:
        @pl.when(first & middle)
        def _():
            sent(piece, 1)

        @pl.when(second & (space == 0) & (stages > 1))
        def _():
            if stages > 2:
                sent(size)
            else:
                sent(size - piece)
                sent(piece, 1)

        @pl.when(hosts)
        def _():
            sent(size)
            sent(size)

        @pl.when(leaps)
        def _():
            sent(size)


def write_out(g, se, out_g, out_se, sems):
    copies = [
        pltpu.make_async_copy(g, out_g.at[:, 0], sems.at[0]),
        pltpu.make_async_copy(se, out_se, sems.at[1]),
    ]
    for copy in copies:
        copy.start()
    for copy in copies:
        copy.wait()


def body(retain, hopping, source, screened):
    slabs, _, _, size, _ = hopping.shape
    energies = screened.shape[1]
    rows = screened.shape[3] // size
    woven = (
        screened.reshape(slabs, energies, 2, rows, size)
        .transpose(0, 1, 3, 2, 4)
        .reshape(slabs, energies, 2 * rows, size)
    )
    any_spec = pl.BlockSpec(memory_space=pl.ANY)
    vmem_spec = pl.BlockSpec(memory_space=pltpu.VMEM)
    vmem = pltpu.VMEM
    greens, self_energy = pl.pallas_call(
        kernel,
        out_shape=(vmem((slabs, 2, size, size), F32), vmem(woven.shape, F32)),
        in_specs=[pl.BlockSpec(memory_space=pltpu.HBM)] * 4,
        out_specs=(vmem_spec, vmem_spec),
        scratch_shapes=[
            pltpu.SMEM((slabs,), F32),
            vmem((2, slabs, 2, size, size), F32),
            vmem(woven.shape, F32),
            vmem((slabs + 1, OUTS, 4 * size // OUTS, 2 * size), BF16),
            vmem((slabs + 1, 2, 2 * size, 2 * size), BF16),
            vmem((slabs, 2 * size, size), F32),
            vmem((2, size, size), F32),
            vmem((slabs, energies, 2, rows, size), F32),
            vmem((2, 2 * size, size), F32),
            vmem((2, 2 * size, size), F32),
            vmem((2, size, size), F32),
            vmem((2, size, size), F32),
            vmem((max(slabs - 1, 1), size, 2 * size), F32),
            pltpu.SemaphoreType.DMA((3,)),
            pltpu.SemaphoreType.DMA((2,)),
            pltpu.SemaphoreType.DMA((GROUPS,)),
            pltpu.SemaphoreType.DMA((GROUPS,)),
            pltpu.SemaphoreType.DMA((1,)),
            pltpu.SemaphoreType.DMA((slabs,)),
            pltpu.SemaphoreType.DMA((2,)),
            pltpu.SemaphoreType.REGULAR,
        ],
        compiler_params=pltpu.CompilerParams(
            collective_id=0, has_side_effects=True
        ),
    )(retain.reshape(slabs), hopping, source, woven)
    greens, self_energy = pl.pallas_call(
        write_out,
        out_shape=(
            jax.ShapeDtypeStruct(source.shape, F32),
            jax.ShapeDtypeStruct(woven.shape, F32),
        ),
        in_specs=[vmem_spec, vmem_spec],
        out_specs=(any_spec, any_spec),
        scratch_shapes=[pltpu.SemaphoreType.DMA((2,))],
        compiler_params=pltpu.CompilerParams(vmem_limit_bytes=4 << 20),
    )(greens, self_energy)
    return greens, (
        self_energy.reshape(slabs, energies, rows, 2, size)
        .transpose(0, 1, 3, 2, 4)
        .reshape(screened.shape)
    )


def solution(mesh):
    placed = (
        P("space", "energy"),
        P("space", "energy", None, None, None),
        P("space", "energy", None, None, None),
        P("space", None, None, "energy"),
    )
    return jax.shard_map(
        body,
        mesh=mesh,
        in_specs=placed,
        out_specs=(P("space", "energy", None, None, None), P("space", None, None, "energy")),
        check_vma=False,
    )
```

time: 18.8 us -> 17.5 us (0.931)
  Pallas kernels: 18 us -> 16.7 us
    pallas_call x1, Pallas kernels: 17.2 us -> 15.9 us  [body(): pl.pallas_call(kernel, out_shape=(vmem((slabs, 2, size, size), F32), vmem...]
where the time goes in v2:
time: 17.5 us; the launch traced here: 17.3 us
  Pallas kernels  16.7 us (95%)
  between operations  0.64 us (4%)
    pallas_call x1, Pallas kernels, body(): pl.pallas_call(kernel, out_shape=(vmem((slabs, 2, size, size), F32), vmem...  15.9 us
    pallas_call x1, Pallas kernels, body(): pl.pallas_call(write_out, out_shape=(jax.ShapeDtypeStruct(source.shape, F...  0.81 us

profile of v2, /device:TPU:17, one launch (start us, length us, event | category | flops | bytes accessed | tf_op | source)
XLA Modules:
  0.0 17.3 jit_solution(12187227622430232234)
XLA Ops:
  0.6 15.9 %shard_map.59 = (f32[2,2,128,128]{3,2,1,0:T(8,128)S(1)}, f32[2,8,32,128]{3,2,1,0:T(8,128)S(1)}) custom-call(f32[2]{0:T(128)} %bitcast.12, f32[2,1,2,128,128]{4,3,2,1,0:T(8,128)} %hop_hbm.1, f32[2,1,2,128,128]{4,3,2,1,0:T(8,128)} %src_hbm.1, f32[2,8,32,128]{3,2,1,0:T(8,128)} %bitcast.11), custom_call_target="tpu_custom_call" | custom-call | tf_op jit(solution)/shard_map/pallas_call | solution.py:524
  16.5 0.8 %shard_map.60 = (f32[2,1,2,128,128]{4,3,2,1,0:T(8,128)}, f32[2,8,32,128]{3,2,1,0:T(8,128)}) custom-call(f32[2,2,128,128]{3,2,1,0:T(8,128)S(1)} %get-tuple-element.6.g, f32[2,8,32,128]{3,2,1,0:T(8,128)S(1)} %get-tuple-element.7.se), custom_call_target="tpu_custom_call" | custom-call | tf_op jit(solution)/shard_map/pallas_call | solution.py:556

commit v3 on v2

--- a/solution.py
+++ b/solution.py
@@ -12,8 +12,9 @@
 BF16 = jnp.bfloat16
 CHUNKS = 8
 GROUPS = 4
-OUTS = 2
-ORDER = {6: 0, 4: 1, 7: 2, 5: 3, 2: 4, 3: 5, 1: 1 << 30}
+OUTS = 4
+ORDER = {6: 0, 7: 1, 4: 2, 5: 3, 2: 4, 3: 5, 1: 1 << 30}
+LS = 4
 
 
 def split(value):
@@ -60,7 +61,14 @@
 
 def part_by(left, right):
     height, size = left.shape[0] // 4, right.shape[1] // 2
-    product = dot(left, right)
+    product = dot(left[: 2 * height], right)
+    other = dot(left[2 * height :], right[:, :size])
+    both = product[:, :size] + (product[:, size:] + other)
+    return both[:height], both[height:]
+
+
+def parts_of(product):
+    height, size = product.shape[0] // 4, product.shape[1] // 2
     cross = product[: 2 * height, size:] + product[2 * height :, :size]
     both = product[: 2 * height, :size] + cross
     return both[:height], both[height:]
@@ -84,7 +92,7 @@
 def kernel(
     retain_hbm, hop_hbm, src_hbm, scr_hbm, g, out_se,
     retain, slabs_in, scr, lefts, rights, bases, entering, landed, own, early, guest, passed, spun,
-    load_sem, chain_send, chain_recv, guest_recv, swap_send, swap_recv, ahead_sem, turn,
+    load_sem, chain_send, chain_recv, guest_recv, swap_send, swap_recv, ahead_sem, turn, ready,
 ):
     _, slabs, _, size, _ = slabs_in.shape
     energies, rows = landed.shape[1], landed.shape[3]
@@ -93,7 +101,7 @@
     piece, height, group = size // CHUNKS, size // OUTS, size // GROUPS
     last = slabs - 1
     paired = energies % 2 == 0
-    power = energies & (energies - 1) == 0 and energies >= OUTS
+    power = energies & (energies - 1) == 0 and paired
     order = sorted(range(1, energies), key=lambda k: ORDER.get(k, k))
     hop, src = slabs_in.at[0], slabs_in.at[1]
 
@@ -116,8 +124,21 @@
 
     loads = [
         pltpu.make_async_copy(retain_hbm, retain, load_sem.at[2]),
-        pltpu.make_async_copy(hop_hbm.at[:, 0], hop, load_sem.at[0]),
-        pltpu.make_async_copy(src_hbm.at[:, 0], src, load_sem.at[0]),
+        *(
+            pltpu.make_async_copy(
+                array.at[which, 0, part, pl.ds(i * size // LS, size // LS)],
+                ref.at[which, part, pl.ds(i * size // LS, size // LS)],
+                load_sem.at[0],
+            )
+            for array, ref, which in (
+                (hop_hbm, hop, slice(1, None)),
+                (src_hbm, src, slice(0, 1)),
+            )
+            for part in range(2)
+            for i in range(LS)
+        ),
+        pltpu.make_async_copy(src_hbm.at[1:, 0], src.at[1:], load_sem.at[3]),
+        pltpu.make_async_copy(hop_hbm.at[:1, 0], hop.at[:1], load_sem.at[3]),
         pltpu.make_async_copy(scr_hbm, scr, load_sem.at[1]),
     ]
     for load in loads:
@@ -128,8 +149,33 @@
     def greet(where, who):
         pl.semaphore_signal(barrier, inc=1, device_id=(where, who), device_id_type=MESH)
 
-    for step in range(1, energies):
-        greet(space, lax.rem(energy + step, energies))
+    bits = [1 << b for b in range(energies.bit_length() - 1)] if power else []
+    rounds = len(bits) - 1
+    if power:
+        for bit in bits:
+            greet(space, jnp.bitwise_xor(energy, bit))
+    else:
+        for step in range(1, energies):
+            greet(space, lax.rem(energy + step, energies))
+
+    def call(level):
+        if 0 < level <= rounds:
+            for bit in bits:
+                pl.semaphore_signal(
+                    ready.at[level - 1],
+                    inc=1,
+                    device_id=(space, jnp.bitwise_xor(energy, bit)),
+                    device_id_type=MESH,
+                )
+
+    def hear(level):
+        if 0 < level <= rounds:
+            pl.semaphore_wait(ready.at[level - 1], len(bits))
+            call(level + 1)
+
+    def hear_all():
+        for level in range(1, rounds + 1):
+            hear(level)
 
     @pl.when((first & (space > 0)) | takes)
     def _():
@@ -153,7 +199,7 @@
             greet(space - 2, partner)
 
     greeted = (
-        energies - 1
+        (len(bits) if power else energies - 1)
         + carries.astype(jnp.int32)
         + hosts.astype(jnp.int32)
         + leaps.astype(jnp.int32)
@@ -162,18 +208,22 @@
 
     def enter():
         pl.semaphore_wait(barrier, greeted)
+        call(1)
 
     loads[0].wait()
-    pltpu.make_async_copy(slabs_in, slabs_in, load_sem.at[0]).wait()
+    pltpu.make_async_copy(hop, hop, load_sem.at[0]).wait()
+
+    def settle():
+        pltpu.make_async_copy(hop, hop, load_sem.at[3]).wait()
 
     eye = (
         lax.broadcasted_iota(jnp.int32, (size, size), 0)
         == lax.broadcasted_iota(jnp.int32, (size, size), 1)
     ).astype(F32)
-    couplers = []
-    for j in range(slabs):
+
+    def coupler(j):
         factor = retain[j]
-        couplers.append((factor * (eye + hop[j, 0]), factor * hop[j, 1]))
+        return factor * (eye + hop[j, 0]), factor * hop[j, 1]
 
     def sandwich(left, right, block):
         wide = jnp.concatenate([block[:size], block[size:]], 1)
@@ -184,10 +234,10 @@
 
     step_lefts, step_rights = [None], [None]
     for j in range(1, slabs):
-        step_lefts.append(arranged(left_form(*couplers[j])))
-        step_rights.append(split(dagger_form(*couplers[j])))
-
-    def copy(source_ref, target_ref, sems, where, who, wait=0):
+        step_lefts.append(arranged(left_form(*coupler(j))))
+        step_rights.append(split(dagger_form(*coupler(j))))
+
+    def copy(source_ref, target_ref, sems, where, who):
         return pltpu.make_async_remote_copy(
             src_ref=source_ref,
             dst_ref=target_ref,
@@ -235,19 +285,16 @@
             peer,
         )
 
-    def spread(j):
+    def spread(*js):
         for k in order:
-            swap(j, jnp.bitwise_xor(energy, k) if power else lax.rem(energy + k, energies)).start()
-
-    def part_spread(j, o):
-        half = energies // OUTS
-        near = [k for k in order if k < half]
-        far = [k for k in order if half <= k]
-        for ks, there in ((near, energy // half == o), (far, energy // half != o)):
-            @pl.when(there)
-            def _():
-                for k in ks:
-                    swap(j, jnp.bitwise_xor(energy, k)).start()
+            if not power:
+                peer = lax.rem(energy + k, energies)
+            elif k == 1:
+                peer = jnp.bitwise_xor(energy, 1)
+            else:
+                peer = jnp.bitwise_xor(energy - lax.rem(energy, 2), k)
+            for j in js:
+                swap(j, peer).start()
 
     def keep(j, block):
         real, imag = block[:size], block[size:]
@@ -268,11 +315,21 @@
     def base_part(j, o):
         return lambda part: bases[j, part * size + o * height : part * size + (o + 1) * height]
 
+    def finish_all(j, inner):
+        whole = jnp.concatenate(left_of(j), 0)
+        product = dot(whole, inner)
+        step = 4 * height
+        for o in range(OUTS):
+            for part, value in enumerate(parts_of(product[o * step : (o + 1) * step])):
+                g[j, part, o * height : (o + 1) * height] = value + base_part(j, o)(part)
+
     def give_turn():
         pl.semaphore_signal(turn, inc=1, device_id=(space, partner), device_id_type=MESH)
 
     @pl.when(space == 0)
     def _():
+        if last > 1:
+            settle()
         base = source(0)
         for j in range(1, slabs):
             g[j - 1, 0] = base[:size]
@@ -281,6 +338,8 @@
                 base = sandwich(step_lefts[j], step_rights[j], base) + source(j)
         wide = jnp.concatenate([base[:size], base[size:]], 1)
         inner = stacked(turned_block(rows_by(wide, step_rights[last])))
+        if last < 2:
+            settle()
         for o in range(OUTS):
             finish(
                 made,
@@ -311,17 +370,18 @@
                 give_turn()
                 pl.semaphore_wait(turn, 1)
 
-        for j in range(last, -1, -1):
-            spread(j)
+        hear_all()
+        spread(*range(last, -1, -1))
 
     @pl.when(space > 0)
     def _():
+        settle()
         base = source(0)
         bases[0] = base
         for j in range(1, slabs):
             base = sandwich(step_lefts[j], step_rights[j], base) + source(j)
             bases[j] = base
-        block = jnp.concatenate(couplers[0], 0)
+        block = jnp.concatenate(coupler(0), 0)
         for j in range(slabs):
             if j > 0:
                 block = columns_by(step_lefts[j], block)
@@ -336,6 +396,15 @@
         @pl.when(gives)
         def _():
             hand(space + 1, energy)
+
+        if paired:
+            @pl.when(hosted & (space == 1))
+            def _():
+                hand(space, partner)
+
+        @pl.when(jnp.logical_not(odd & middle))
+        def _():
+            hear_all()
 
         @pl.when(takes)
         def _():
@@ -352,41 +421,44 @@
                         own[1] = bases[last]
 
         if paired:
-            @pl.when(hosted)
+            @pl.when(hosted & (space > 1))
             def _():
                 hand(space, partner)
 
+        for c in range(GROUPS):
+            line(made, entering, chain_recv, c * group, group, space, energy).wait_recv()
+            lines = pl.ds(c * group, group)
+            arrived = jnp.concatenate([entering[0, lines], entering[1, lines]], 1)
+            if c < GROUPS - 1:
+                for j in range(last, -1, -1):
+                    spun[j, lines] = rows_by(arrived, right_of(j))
+
+        def inner_of(j):
+            tail = rows_by(arrived, right_of(j))
+            return stacked(turned_block(jnp.concatenate([spun[j, : size - group], tail], 0)))
+
+        @pl.when(stops)
+        def _():
+            inners = [inner_of(j) for j in range(slabs)]
+            for j in range(last, -1, -1):
+                finish_all(j, inners[j])
+            spread(*range(last, -1, -1))
+
+        @pl.when(jnp.logical_not(stops))
+        def _():
+            inner = inner_of(last)
+            for o in range(OUTS):
+                finish(made, o, lefts[last, o], inner, base_part(last, o))
+
+                @pl.when(first)
+                def _():
+                    send_on(o * CHUNKS // OUTS, CHUNKS // OUTS)
+
+        if paired:
             @pl.when(hosts)
             def _():
                 ahead((own, early), space, energy).wait_recv()
                 keep(slabs, early[0])
-
-        turned = []
-        for c in range(GROUPS):
-            line(made, entering, chain_recv, c * group, group, space, energy).wait_recv()
-            lines = pl.ds(c * group, group)
-            arrived = jnp.concatenate([entering[0, lines], entering[1, lines]], 1)
-            turned.append(rows_by(arrived, right_of(last)))
-            if c < GROUPS - 1:
-                for j in range(last):
-                    spun[j, lines] = rows_by(arrived, right_of(j))
-
-        inner = stacked(turned_block(jnp.concatenate(turned, 0)))
-        for o in range(OUTS):
-            finish(made, o, lefts[last, o], inner, base_part(last, o))
-
-            @pl.when(middle & first)
-            def _():
-                send_on(o * CHUNKS // OUTS, CHUNKS // OUTS)
-
-            if power:
-                @pl.when(stops)
-                def _():
-                    part_spread(last, o)
-
-        if paired:
-            @pl.when(hosts)
-            def _():
                 turned = []
                 for c in range(GROUPS):
                     line(made, guest, guest_recv, c * group, group, space, energy).wait_recv()
@@ -427,25 +499,22 @@
             def _():
                 pl.semaphore_wait(turn, 1)
 
-        @pl.when(jnp.logical_not(stops) if power else True)
+        @pl.when(odd & middle)
+        def _():
+            hear_all()
+
+        @pl.when(jnp.logical_not(stops))
         def _():
             spread(last)
-
-        for j in range(last - 1, -1, -1):
-            tail = pl.ds(size - group, group)
-            spun[j, tail] = rows_by(arrived, right_of(j))
-            inner = stacked(turned_block(spun[j]))
-            for o in range(OUTS):
-                finish(g.at[j], o, lefts[j, o], inner, base_part(j, o))
-                if power:
-                    part_spread(j, o)
-            if not power:
+            for j in range(last - 1, -1, -1):
+                inner = inner_of(j)
+                finish_all(j, inner)
                 spread(j)
 
     def lanes(part):
         return pl.ds(part, rows, stride=2)
 
-    loads[3].wait()
+    loads[-1].wait()
     mine = pl.ds(pl.multiple_of(energy * rows, rows), rows)
     for j in range(last, -1, -1):
         landed[j, energy] = g[j, :, mine]
@@ -539,8 +608,8 @@
             vmem((2, 2 * size, size), F32),
             vmem((2, size, size), F32),
             vmem((2, size, size), F32),
-            vmem((max(slabs - 1, 1), size, 2 * size), F32),
-            pltpu.SemaphoreType.DMA((3,)),
+            vmem((slabs, size, 2 * size), F32),
+            pltpu.SemaphoreType.DMA((4,)),
             pltpu.SemaphoreType.DMA((2,)),
             pltpu.SemaphoreType.DMA((GROUPS,)),
             pltpu.SemaphoreType.DMA((GROUPS,)),
@@ -548,6 +617,7 @@
             pltpu.SemaphoreType.DMA((slabs,)),
             pltpu.SemaphoreType.DMA((2,)),
             pltpu.SemaphoreType.REGULAR,
+            pltpu.SemaphoreType.REGULAR((max(energies.bit_length() - 2, 1),)),
         ],
         compiler_params=pltpu.CompilerParams(
             collective_id=0, has_side_effects=True

time: 17.5 us -> 17 us (0.971)
  Pallas kernels: 16.7 us -> 16.2 us
    pallas_call x1, Pallas kernels: 15.9 us -> 15.4 us  [body(): pl.pallas_call(kernel, out_shape=(vmem((slabs, 2, size, size), F32), vmem...]
where the time goes in v3:
time: 17 us; the launch traced here: 16.8 us
  Pallas kernels  16.2 us (95%)
  between operations  0.64 us (4%)
    pallas_call x1, Pallas kernels, body(): pl.pallas_call(kernel, out_shape=(vmem((slabs, 2, size, size), F32), vmem...  15.4 us
    pallas_call x1, Pallas kernels, body(): pl.pallas_call(write_out, out_shape=(jax.ShapeDtypeStruct(source.shape, F...  0.81 us

profile of v3, /device:TPU:17, one launch (start us, length us, event | category | flops | bytes accessed | tf_op | source)
XLA Modules:
  0.0 16.8 jit_solution(11333736640693418186)
XLA Ops:
  0.6 15.4 %shard_map.59 = (f32[2,2,128,128]{3,2,1,0:T(8,128)S(1)}, f32[2,8,32,128]{3,2,1,0:T(8,128)S(1)}) custom-call(f32[2]{0:T(128)} %bitcast.12, f32[2,1,2,128,128]{4,3,2,1,0:T(8,128)} %hop_hbm.1, f32[2,1,2,128,128]{4,3,2,1,0:T(8,128)} %src_hbm.1, f32[2,8,32,128]{3,2,1,0:T(8,128)} %bitcast.11), custom_call_target="tpu_custom_call" | custom-call | tf_op jit(solution)/shard_map/pallas_call | solution.py:593
  16.0 0.8 %shard_map.60 = (f32[2,1,2,128,128]{4,3,2,1,0:T(8,128)}, f32[2,8,32,128]{3,2,1,0:T(8,128)}) custom-call(f32[2,2,128,128]{3,2,1,0:T(8,128)S(1)} %get-tuple-element.6.g, f32[2,8,32,128]{3,2,1,0:T(8,128)S(1)} %get-tuple-element.7.se), custom_call_target="tpu_custom_call" | custom-call | tf_op jit(solution)/shard_map/pallas_call | solution.py:626

commit v4 on v3

--- a/solution.py
+++ b/solution.py
@@ -91,7 +91,7 @@
 
 def kernel(
     retain_hbm, hop_hbm, src_hbm, scr_hbm, g, out_se,
-    retain, slabs_in, scr, lefts, rights, bases, entering, landed, own, early, guest, passed, spun,
+    retain, slabs_in, scr, lefts, rights, bases, entering, landed, own, brought, early, guest, passed, spun,
     load_sem, chain_send, chain_recv, guest_recv, swap_send, swap_recv, ahead_sem, turn, ready,
 ):
     _, slabs, _, size, _ = slabs_in.shape
@@ -102,11 +102,14 @@
     last = slabs - 1
     paired = energies % 2 == 0
     power = energies & (energies - 1) == 0 and paired
+    per = energies // OUTS
+    quartered = power and per >= 2
     order = sorted(range(1, energies), key=lambda k: ORDER.get(k, k))
     hop, src = slabs_in.at[0], slabs_in.at[1]
 
     odd = lax.rem(space, 2) == 1
     middle = (space > 0) & (space < stages - 1)
+    paired = paired and power
     if paired:
         partner = energy + 1 - 2 * lax.rem(energy, 2)
         second = lax.rem(energy, 2) == 0
@@ -114,13 +117,12 @@
         partner = energy
         second = energy < 0
     first = jnp.logical_not(second)
-    hosts = first & odd & middle & paired
-    hosted = second & odd & middle
+    hosts = first & (space > 0) & paired
+    hosted = second & (space > 0)
     gives = second & middle & jnp.logical_not(odd)
-    takes = second & odd & (space > 1)
-    leaps = hosts & (space + 2 < stages)
-    carries = (first & (space < stages - 1)) | (second & (space == 0) & (stages > 1))
-    stops = (space == stages - 1) | gives
+    takes = hosts & odd & (space > 1)
+    links = hosts & odd & middle
+    leaps = links & (space + 2 < stages)
 
     loads = [
         pltpu.make_async_copy(retain_hbm, retain, load_sem.at[2]),
@@ -177,33 +179,24 @@
         for level in range(1, rounds + 1):
             hear(level)
 
-    @pl.when((first & (space > 0)) | takes)
+    @pl.when(first & (space > 0))
     def _():
         greet(space - 1, energy)
 
     if paired:
-        @pl.when(((space == 1) & hosts) | (second & (space > 0) & jnp.logical_not(odd)))
+        @pl.when((hosts & (space == 1)) | takes)
         def _():
             greet(space - 1, partner)
 
-        @pl.when((space == 1) & second & (stages == 2))
-        def _():
-            greet(space - 1, energy)
-
-        @pl.when(hosts & (space > 1))
+        @pl.when(takes)
         def _():
             greet(space - 2, energy)
-
-        @pl.when(takes & (space == stages - 1))
-        def _():
-            greet(space - 2, partner)
 
     greeted = (
         (len(bits) if power else energies - 1)
-        + carries.astype(jnp.int32)
-        + hosts.astype(jnp.int32)
+        + (first & (space < stages - 1)).astype(jnp.int32)
         + leaps.astype(jnp.int32)
-        + gives.astype(jnp.int32)
+        + (second & (space < stages - 1) & jnp.logical_not(odd)).astype(jnp.int32)
     )
 
     def enter():
@@ -269,21 +262,36 @@
     def sent(count, sem=0):
         line(made, entering, chain_recv, 0, count, space, energy, sem=sem).wait_send()
 
-    def ahead(refs, where, who):
-        return copy(refs[0], refs[1], (ahead_sem.at[0], ahead_sem.at[1]), where, who)
-
-    def hand(where, who):
-        for i in range(2):
-            ahead((own.at[i], early.at[i]), where, who).start()
-
-    def swap(j, peer):
+    def ahead(where, who):
+        return [
+            copy(
+                own.at[i * slabs + last], early.at[i], (ahead_sem.at[0], ahead_sem.at[1]), where, who
+            )
+            for i in range(2)
+        ]
+
+    def aheads():
+        return copy(early, early, (ahead_sem.at[0], ahead_sem.at[1]), space, energy)
+
+    def bring(refs=None):
+        return copy(own, brought, (ahead_sem.at[0], ahead_sem.at[2]), space, partner)
+
+    def swap(j, peer, source=None, who=None):
+        rows_of = pl.ds(pl.multiple_of(peer * rows, rows), rows)
         return copy(
-            g.at[j, :, pl.ds(pl.multiple_of(peer * rows, rows), rows)],
-            landed.at[j, energy],
+            (g if source is None else source).at[j, :, rows_of],
+            landed.at[j, energy if who is None else who],
             (swap_send.at[0], swap_recv.at[j]),
             space,
             peer,
         )
+
+    def spread_guest(*js):
+        for k in order:
+            if k > 1:
+                peer = jnp.bitwise_xor(energy - lax.rem(energy, 2), k)
+                for j in js:
+                    swap(j, peer, passed, partner).start()
 
     def spread(*js):
         for k in order:
@@ -315,13 +323,19 @@
     def base_part(j, o):
         return lambda part: bases[j, part * size + o * height : part * size + (o + 1) * height]
 
-    def finish_all(j, inner):
+    def finish_all(j, inner, target=None, more=None):
         whole = jnp.concatenate(left_of(j), 0)
         product = dot(whole, inner)
         step = 4 * height
         for o in range(OUTS):
             for part, value in enumerate(parts_of(product[o * step : (o + 1) * step])):
-                g[j, part, o * height : (o + 1) * height] = value + base_part(j, o)(part)
+                start = part * size + o * height
+                if target is None:
+                    g[j, part, o * height : (o + 1) * height] = value + base_part(j, o)(part)
+                else:
+                    target[part, o * height : (o + 1) * height] = (
+                        value + more[start : start + height]
+                    )
 
     def give_turn():
         pl.semaphore_signal(turn, inc=1, device_id=(space, partner), device_id_type=MESH)
@@ -341,12 +355,13 @@
         if last < 2:
             settle()
         for o in range(OUTS):
+            lines = slice(o * height, (o + 1) * height)
             finish(
                 made,
                 o,
                 step_lefts[last][o],
                 inner,
-                lambda part: src[last, part, o * height : (o + 1) * height],
+                lambda part: src[last, part, lines],
             )
             if o == 0:
                 enter()
@@ -358,10 +373,7 @@
             @pl.when(second)
             def _():
                 pl.semaphore_wait(turn, 1)
-                if stages > 2:
-                    send_on(0, CHUNKS, True)
-                else:
-                    send_on(0, CHUNKS)
+                send_on(0, CHUNKS, True)
                 give_turn()
 
             @pl.when(first)
@@ -387,129 +399,170 @@
                 block = columns_by(step_lefts[j], block)
             keep(j, block)
 
-        @pl.when(gives | (hosted & (space == 1)))
-        def _():
-            own[0] = block
-            own[1] = bases[last]
+            own[j] = block
+            own[slabs + j] = bases[j]
         enter()
 
-        @pl.when(gives)
-        def _():
-            hand(space + 1, energy)
-
         if paired:
-            @pl.when(hosted & (space == 1))
-            def _():
-                hand(space, partner)
-
-        @pl.when(jnp.logical_not(odd & middle))
+            @pl.when(hosted)
+            def _():
+                bring().start()
+
+            @pl.when(gives)
+            def _():
+                for part in ahead(space + 1, partner):
+                    part.start()
+
+        @pl.when(hosted | jnp.logical_not(odd & middle))
         def _():
             hear_all()
 
-        @pl.when(takes)
-        def _():
-            ahead((own, early), space, energy).wait_recv()
+        def gather(source_ref, recv, begin):
+            for c in range(GROUPS):
+                line(made, source_ref, recv, c * group, group, space, energy).wait_recv()
+                if c < GROUPS - 1:
+                    lines = pl.ds(c * group, group)
+                    arrived = jnp.concatenate([source_ref[0, lines], source_ref[1, lines]], 1)
+                    for j in range(last, -1, -1):
+                        spun[begin + j, lines] = rows_by(arrived, right_of(begin + j))
+
+        def inner_of(source_ref, begin, j):
+            lines = pl.ds(size - group, group)
+            arrived = jnp.concatenate([source_ref[0, lines], source_ref[1, lines]], 1)
+            tail = rows_by(arrived, right_of(begin + j))
+            return stacked(turned_block(jnp.concatenate([spun[begin + j, : size - group], tail], 0)))
+
+        def own_part():
+            gather(entering, chain_recv, 0)
+
+            @pl.when(space == stages - 1)
+            def _():
+                inners = [inner_of(entering, 0, j) for j in range(slabs)]
+                if quartered:
+                    for d in range(OUTS - 1, -1, -1):
+                        o = jnp.bitwise_xor(energy // per, d)
+                        for j in range(last, -1, -1):
+                            for part, value in enumerate(part_by(lefts[j, o], inners[j])):
+                                at = pl.multiple_of(o * height, height)
+                                g[j, part, pl.ds(at, height)] = (
+                                    value + bases[j, pl.ds(part * size + at, height)]
+                                )
+                        for i in range(0 if d else 1, per):
+                            peer = o * per + i if d else jnp.bitwise_xor(energy, i)
+                            for j in range(last, -1, -1):
+                                swap(j, peer).start()
+                else:
+                    for j in range(last, -1, -1):
+                        finish_all(j, inners[j])
+                    spread(*range(last, -1, -1))
+
+            @pl.when(middle)
+            def _():
+                inner = inner_of(entering, 0, last)
+                for o in range(OUTS):
+                    finish(made, o, lefts[last, o], inner, base_part(last, o))
+                    send_on(o * CHUNKS // OUTS, CHUNKS // OUTS)
+
+        def own_rest():
+            @pl.when(middle)
+            def _():
+                for j in range(last - 1, -1, -1):
+                    finish_all(j, inner_of(entering, 0, j))
+
+        def welcome():
+            bring().wait_recv()
             for j in range(slabs):
-                left = left_of(j)
-                bases[j] = sandwich(left, right_of(j), early[1]) + bases[j]
-                block = columns_by(left, early[0])
-                keep(j, block)
-                if j == last:
-                    @pl.when(hosted)
-                    def _():
-                        own[0] = block
-                        own[1] = bases[last]
-
-        if paired:
-            @pl.when(hosted & (space > 1))
-            def _():
-                hand(space, partner)
-
-        for c in range(GROUPS):
-            line(made, entering, chain_recv, c * group, group, space, energy).wait_recv()
-            lines = pl.ds(c * group, group)
-            arrived = jnp.concatenate([entering[0, lines], entering[1, lines]], 1)
-            if c < GROUPS - 1:
+                keep(slabs + j, brought[j])
+
+        def guest_part():
+            gather(guest, guest_recv, slabs)
+
+            @pl.when(jnp.logical_not(odd & middle))
+            def _():
+                inners = [inner_of(guest, slabs, j) for j in range(slabs)]
                 for j in range(last, -1, -1):
-                    spun[j, lines] = rows_by(arrived, right_of(j))
-
-        def inner_of(j):
-            tail = rows_by(arrived, right_of(j))
-            return stacked(turned_block(jnp.concatenate([spun[j, : size - group], tail], 0)))
-
-        @pl.when(stops)
-        def _():
-            inners = [inner_of(j) for j in range(slabs)]
-            for j in range(last, -1, -1):
-                finish_all(j, inners[j])
-            spread(*range(last, -1, -1))
-
-        @pl.when(jnp.logical_not(stops))
-        def _():
-            inner = inner_of(last)
-            for o in range(OUTS):
-                finish(made, o, lefts[last, o], inner, base_part(last, o))
-
-                @pl.when(first)
-                def _():
-                    send_on(o * CHUNKS // OUTS, CHUNKS // OUTS)
-
-        if paired:
-            @pl.when(hosts)
-            def _():
-                ahead((own, early), space, energy).wait_recv()
-                keep(slabs, early[0])
-                turned = []
-                for c in range(GROUPS):
-                    line(made, guest, guest_recv, c * group, group, space, energy).wait_recv()
-                    line(guest, entering, chain_recv, c * group, group, space, partner).start()
-                    lines = pl.ds(c * group, group)
-                    arrived = jnp.concatenate([guest[0, lines], guest[1, lines]], 1)
-                    turned.append(rows_by(arrived, right_of(slabs)))
-                inner = stacked(turned_block(jnp.concatenate(turned, 0)))
+                    finish_all(slabs + j, inners[j], passed.at[j], brought.at[slabs + j])
+                spread_guest(*range(last, -1, -1))
+                copy(passed, g, (chain_send.at[0], chain_recv.at[0]), space, partner).start()
+
+            @pl.when(odd & middle)
+            def _():
+                inner = inner_of(guest, slabs, last)
+                out = passed.at[last]
                 for o in range(OUTS):
                     finish(
-                        passed,
+                        out,
                         o,
-                        lefts[slabs, o],
+                        lefts[slabs + last, o],
                         inner,
-                        lambda part: early[
-                            1, part * size + o * height : part * size + (o + 1) * height
+                        lambda part: brought[
+                            slabs + last,
+                            part * size + o * height : part * size + (o + 1) * height,
                         ],
                     )
-                    chunks = range(o * CHUNKS // OUTS, (o + 1) * CHUNKS // OUTS)
-
-                    @pl.when(leaps & (space + 2 < stages - 1))
+
+                    @pl.when(leaps)
                     def _():
-                        for c in chunks:
-                            line(passed, guest, guest_recv, c * piece, piece, space + 2, energy).start()
-
-                    @pl.when(leaps & (space + 2 == stages - 1))
-                    def _():
-                        for c in chunks:
-                            line(
-                                passed, entering, chain_recv, c * piece, piece, space + 2, partner
-                            ).start()
+                        for c in range(o * CHUNKS // OUTS, (o + 1) * CHUNKS // OUTS):
+                            line(out, guest, guest_recv, c * piece, piece, space + 2, energy).start()
 
                 for c in range(CHUNKS):
-                    line(passed, entering, chain_recv, c * piece, piece, space + 1, partner).start()
-                give_turn()
+                    line(out, guest, guest_recv, c * piece, piece, space + 1, energy).start()
+                for j in range(last - 1, -1, -1):
+                    finish_all(
+                        slabs + j, inner_of(guest, slabs, j), passed.at[j], brought.at[slabs + j]
+                    )
+                copy(passed, g, (chain_send.at[0], chain_recv.at[0]), space, partner).start()
+
+        if not paired:
+            own_part()
+            own_rest()
+            @pl.when(middle)
+            def _():
+                spread(*range(last, -1, -1))
+        else:
+            @pl.when(takes)
+            def _():
+                welcome()
+                aheads().wait_recv()
+                for j in range(slabs):
+                    left = left_of(slabs + j)
+                    brought[slabs + j] = (
+                        sandwich(left, right_of(slabs + j), early[1]) + brought[slabs + j]
+                    )
+                    keep(slabs + j, columns_by(left, early[0]))
+                guest_part()
+
+            @pl.when(first)
+            def _():
+                own_part()
+
+            @pl.when(first & middle & jnp.logical_not(odd))
+            def _():
+                own_rest()
+                spread(*range(last, -1, -1))
+
+            @pl.when(hosts & jnp.logical_not(takes))
+            def _():
+                welcome()
+                guest_part()
+
+            @pl.when(links)
+            def _():
+                hear_all()
+                spread(last)
+                own_rest()
+                spread(*range(last - 1, -1, -1))
+                spread_guest(*range(last, -1, -1))
+
+            @pl.when(hosts)
+            def _():
+                for j in range(slabs):
+                    landed[j, partner] = passed[j, :, pl.ds(pl.multiple_of(energy * rows, rows), rows)]
 
             @pl.when(hosted)
             def _():
-                pl.semaphore_wait(turn, 1)
-
-        @pl.when(odd & middle)
-        def _():
-            hear_all()
-
-        @pl.when(jnp.logical_not(stops))
-        def _():
-            spread(last)
-            for j in range(last - 1, -1, -1):
-                inner = inner_of(j)
-                finish_all(j, inner)
-                spread(j)
+                copy(passed, g, (chain_send.at[0], chain_recv.at[0]), space, energy).wait_recv()
 
     def lanes(part):
         return pl.ds(part, rows, stride=2)
@@ -518,8 +571,11 @@
     mine = pl.ds(pl.multiple_of(energy * rows, rows), rows)
     for j in range(last, -1, -1):
         landed[j, energy] = g[j, :, mine]
-        others = landed.at[j, pl.ds(0, energies - 1)]
-        pltpu.make_async_copy(others, others, swap_recv.at[j]).wait()
+        for count, there in ((energies - 2, hosts), (energies - 1, jnp.logical_not(hosts))):
+            @pl.when(there)
+            def _():
+                others = landed.at[j, pl.ds(0, count)]
+                pltpu.make_async_copy(others, others, swap_recv.at[j]).wait()
         for e in range(energies):
             real = jnp.zeros((rows, size), F32)
             imag = jnp.zeros((rows, size), F32)
@@ -532,11 +588,11 @@
             out_se[j, e, lanes(1)] = imag
 
     others = landed.at[:, pl.ds(0, energies - 1)]
-    pltpu.make_async_copy(others, others, swap_send.at[0]).wait()
-
-    @pl.when(gives | hosted)
+    fewer = landed.at[:, pl.ds(0, energies - 2)]
+
+    @pl.when(jnp.logical_not(hosted))
     def _():
-        ahead((own, early), space, energy).wait_send()
+        pltpu.make_async_copy(others, others, swap_send.at[0]).wait()
 
     @pl.when(first & (space < stages - 1))
     def _():
@@ -549,17 +605,25 @@
         def _():
             sent(piece, 1)
 
+        @pl.when(hosted)
+        def _():
+            bring().wait_send()
+
+        @pl.when(gives)
+        def _():
+            aheads().wait_send()
+
         @pl.when(second & (space == 0) & (stages > 1))
         def _():
-            if stages > 2:
-                sent(size)
-            else:
-                sent(size - piece)
-                sent(piece, 1)
+            sent(size)
 
         @pl.when(hosts)
         def _():
-            sent(size)
+            pltpu.make_async_copy(fewer, fewer, swap_send.at[0]).wait()
+            copy(passed, g, (chain_send.at[0], chain_recv.at[0]), space, partner).wait_send()
+
+        @pl.when(links)
+        def _():
             sent(size)
 
         @pl.when(leaps)
@@ -599,23 +663,24 @@
             pltpu.SMEM((slabs,), F32),
             vmem((2, slabs, 2, size, size), F32),
             vmem(woven.shape, F32),
-            vmem((slabs + 1, OUTS, 4 * size // OUTS, 2 * size), BF16),
-            vmem((slabs + 1, 2, 2 * size, 2 * size), BF16),
+            vmem((2 * slabs, OUTS, 4 * size // OUTS, 2 * size), BF16),
+            vmem((2 * slabs, 2, 2 * size, 2 * size), BF16),
             vmem((slabs, 2 * size, size), F32),
             vmem((2, size, size), F32),
             vmem((slabs, energies, 2, rows, size), F32),
-            vmem((2, 2 * size, size), F32),
+            vmem((2 * slabs, 2 * size, size), F32),
+            vmem((2 * slabs, 2 * size, size), F32),
             vmem((2, 2 * size, size), F32),
             vmem((2, size, size), F32),
-            vmem((2, size, size), F32),
-            vmem((slabs, size, 2 * size), F32),
+            vmem((slabs, 2, size, size), F32),
+            vmem((2 * slabs, size, 2 * size), F32),
             pltpu.SemaphoreType.DMA((4,)),
             pltpu.SemaphoreType.DMA((2,)),
             pltpu.SemaphoreType.DMA((GROUPS,)),
             pltpu.SemaphoreType.DMA((GROUPS,)),
             pltpu.SemaphoreType.DMA((1,)),
             pltpu.SemaphoreType.DMA((slabs,)),
-            pltpu.SemaphoreType.DMA((2,)),
+            pltpu.SemaphoreType.DMA((3,)),
             pltpu.SemaphoreType.REGULAR,
             pltpu.SemaphoreType.REGULAR((max(energies.bit_length() - 2, 1),)),
         ],

time: 17 us -> 16.4 us (0.965)
  Pallas kernels: 16.2 us -> 15.6 us
    pallas_call x1, Pallas kernels: 15.4 us -> 14.8 us  [body(): pl.pallas_call(kernel, out_shape=(vmem((slabs, 2, size, size), F32), vmem...]
where the time goes in v4:
time: 16.4 us; the launch traced here: 16.2 us
  Pallas kernels  15.6 us (95%)
  between operations  0.64 us (4%)
    pallas_call x1, Pallas kernels, body(): pl.pallas_call(kernel, out_shape=(vmem((slabs, 2, size, size), F32), vmem...  14.8 us
    pallas_call x1, Pallas kernels, body(): pl.pallas_call(write_out, out_shape=(jax.ShapeDtypeStruct(source.shape, F...  0.81 us

profile of v4, /device:TPU:17, one launch (start us, length us, event | category | flops | bytes accessed | tf_op | source)
XLA Modules:
  0.0 16.2 jit_solution(17295539681472405665)
XLA Ops:
  0.6 14.8 %shard_map.59 = (f32[2,2,128,128]{3,2,1,0:T(8,128)S(1)}, f32[2,8,32,128]{3,2,1,0:T(8,128)S(1)}) custom-call(f32[2]{0:T(128)} %bitcast.12, f32[2,1,2,128,128]{4,3,2,1,0:T(8,128)} %hop_hbm.1, f32[2,1,2,128,128]{4,3,2,1,0:T(8,128)} %src_hbm.1, f32[2,8,32,128]{3,2,1,0:T(8,128)} %bitcast.11), custom_call_target="tpu_custom_call" | custom-call | tf_op jit(solution)/shard_map/pallas_call | solution.py:657
  15.4 0.8 %shard_map.60 = (f32[2,1,2,128,128]{4,3,2,1,0:T(8,128)}, f32[2,8,32,128]{3,2,1,0:T(8,128)}) custom-call(f32[2,2,128,128]{3,2,1,0:T(8,128)S(1)} %get-tuple-element.6.g, f32[2,8,32,128]{3,2,1,0:T(8,128)S(1)} %get-tuple-element.7.se), custom_call_target="tpu_custom_call" | custom-call | tf_op jit(solution)/shard_map/pallas_call | solution.py:691

commit v5 on v4

--- a/solution.py
+++ b/solution.py
@@ -90,8 +90,8 @@
 
 
 def kernel(
-    retain_hbm, hop_hbm, src_hbm, scr_hbm, g, out_se,
-    retain, slabs_in, scr, lefts, rights, bases, entering, landed, own, brought, early, guest, passed, spun,
+    retain_hbm, hop_hbm, src_hbm, scr_hbm, g, landed, scr,
+    retain, slabs_in, lefts, rights, bases, entering, own, brought, early, guest, passed, spun,
     load_sem, chain_send, chain_recv, guest_recv, swap_send, swap_recv, ahead_sem, turn, ready,
 ):
     _, slabs, _, size, _ = slabs_in.shape
@@ -262,18 +262,15 @@
     def sent(count, sem=0):
         line(made, entering, chain_recv, 0, count, space, energy, sem=sem).wait_send()
 
-    def ahead(where, who):
-        return [
-            copy(
-                own.at[i * slabs + last], early.at[i], (ahead_sem.at[0], ahead_sem.at[1]), where, who
-            )
-            for i in range(2)
-        ]
+    def ahead(i, where, who):
+        return copy(
+            own.at[i * slabs + last], early.at[i], (ahead_sem.at[0], ahead_sem.at[1]), where, who
+        )
 
     def aheads():
         return copy(early, early, (ahead_sem.at[0], ahead_sem.at[1]), space, energy)
 
-    def bring(refs=None):
+    def bring():
         return copy(own, brought, (ahead_sem.at[0], ahead_sem.at[2]), space, partner)
 
     def swap(j, peer, source=None, who=None):
@@ -336,6 +333,23 @@
                     target[part, o * height : (o + 1) * height] = (
                         value + more[start : start + height]
                     )
+
+    def quarters(begin, inners, target, more, source_ref, who):
+        for d in range(OUTS - 1, -1, -1):
+            o = jnp.bitwise_xor(energy // per, d)
+            at = pl.multiple_of(o * height, height)
+            for j in range(last, -1, -1):
+                for part, value in enumerate(part_by(lefts[begin + j, o], inners[j])):
+                    target[j, part, pl.ds(at, height)] = (
+                        value + more[begin + j, pl.ds(part * size + at, height)]
+                    )
+            if d:
+                peers = [o * per + i for i in range(per)]
+            else:
+                peers = [jnp.bitwise_xor(energy, i) for i in range(2 if begin else 1, per)]
+            for peer in peers:
+                for j in range(last, -1, -1):
+                    swap(j, peer, source_ref, who).start()
 
     def give_turn():
         pl.semaphore_signal(turn, inc=1, device_id=(space, partner), device_id_type=MESH)
@@ -388,30 +402,34 @@
     @pl.when(space > 0)
     def _():
         settle()
-        base = source(0)
-        bases[0] = base
-        for j in range(1, slabs):
-            base = sandwich(step_lefts[j], step_rights[j], base) + source(j)
-            bases[j] = base
         block = jnp.concatenate(coupler(0), 0)
         for j in range(slabs):
             if j > 0:
                 block = columns_by(step_lefts[j], block)
             keep(j, block)
-
             own[j] = block
-            own[slabs + j] = bases[j]
         enter()
 
         if paired:
+            @pl.when(gives)
+            def _():
+                ahead(0, space + 1, partner).start()
+
+        base = source(0)
+        bases[0] = base
+        own[slabs] = base
+        for j in range(1, slabs):
+            base = sandwich(step_lefts[j], step_rights[j], base) + source(j)
+            bases[j] = base
+            own[slabs + j] = base
+        if paired:
+            @pl.when(gives)
+            def _():
+                ahead(1, space + 1, partner).start()
+
             @pl.when(hosted)
             def _():
                 bring().start()
-
-            @pl.when(gives)
-            def _():
-                for part in ahead(space + 1, partner):
-                    part.start()
 
         @pl.when(hosted | jnp.logical_not(odd & middle))
         def _():
@@ -439,18 +457,7 @@
             def _():
                 inners = [inner_of(entering, 0, j) for j in range(slabs)]
                 if quartered:
-                    for d in range(OUTS - 1, -1, -1):
-                        o = jnp.bitwise_xor(energy // per, d)
-                        for j in range(last, -1, -1):
-                            for part, value in enumerate(part_by(lefts[j, o], inners[j])):
-                                at = pl.multiple_of(o * height, height)
-                                g[j, part, pl.ds(at, height)] = (
-                                    value + bases[j, pl.ds(part * size + at, height)]
-                                )
-                        for i in range(0 if d else 1, per):
-                            peer = o * per + i if d else jnp.bitwise_xor(energy, i)
-                            for j in range(last, -1, -1):
-                                swap(j, peer).start()
+                    quarters(0, inners, g, bases, None, None)
                 else:
                     for j in range(last, -1, -1):
                         finish_all(j, inners[j])
@@ -480,9 +487,12 @@
             @pl.when(jnp.logical_not(odd & middle))
             def _():
                 inners = [inner_of(guest, slabs, j) for j in range(slabs)]
-                for j in range(last, -1, -1):
-                    finish_all(slabs + j, inners[j], passed.at[j], brought.at[slabs + j])
-                spread_guest(*range(last, -1, -1))
+                if quartered:
+                    quarters(slabs, inners, passed, brought, passed, partner)
+                else:
+                    for j in range(last, -1, -1):
+                        finish_all(slabs + j, inners[j], passed.at[j], brought.at[slabs + j])
+                    spread_guest(*range(last, -1, -1))
                 copy(passed, g, (chain_send.at[0], chain_recv.at[0]), space, partner).start()
 
             @pl.when(odd & middle)
@@ -564,9 +574,6 @@
             def _():
                 copy(passed, g, (chain_send.at[0], chain_recv.at[0]), space, energy).wait_recv()
 
-    def lanes(part):
-        return pl.ds(part, rows, stride=2)
-
     loads[-1].wait()
     mine = pl.ds(pl.multiple_of(energy * rows, rows), rows)
     for j in range(last, -1, -1):
@@ -576,6 +583,59 @@
             def _():
                 others = landed.at[j, pl.ds(0, count)]
                 pltpu.make_async_copy(others, others, swap_recv.at[j]).wait()
+
+    others = landed.at[:, pl.ds(0, energies - 1)]
+    fewer = landed.at[:, pl.ds(0, energies - 2)]
+
+    @pl.when(jnp.logical_not(hosted))
+    def _():
+        pltpu.make_async_copy(others, others, swap_send.at[0]).wait()
+
+    @pl.when(first & (space < stages - 1))
+    def _():
+        sent(size - piece)
+        if not paired:
+            sent(piece, 1)
+
+    if paired:
+        @pl.when(first & middle)
+        def _():
+            sent(piece, 1)
+
+        @pl.when(hosted)
+        def _():
+            bring().wait_send()
+
+        @pl.when(gives)
+        def _():
+            aheads().wait_send()
+
+        @pl.when(second & (space == 0) & (stages > 1))
+        def _():
+            sent(size)
+
+        @pl.when(hosts)
+        def _():
+            pltpu.make_async_copy(fewer, fewer, swap_send.at[0]).wait()
+            copy(passed, g, (chain_send.at[0], chain_recv.at[0]), space, partner).wait_send()
+
+        @pl.when(links)
+        def _():
+            sent(size)
+
+        @pl.when(leaps)
+        def _():
+            sent(size)
+
+
+def write_out(g, landed, scr, out_g, out_se, se, sems):
+    slabs, energies, _, rows, size = landed.shape
+
+    def lanes(part):
+        return pl.ds(part, rows, stride=2)
+
+    pltpu.make_async_copy(g, out_g.at[:, 0], sems.at[0]).start()
+    for j in range(slabs):
         for e in range(energies):
             real = jnp.zeros((rows, size), F32)
             imag = jnp.zeros((rows, size), F32)
@@ -584,62 +644,11 @@
                 sr, si = scr[j, w, lanes(0)], scr[j, w, lanes(1)]
                 real = real + (gr * sr - gi * si)
                 imag = imag + (gr * si + gi * sr)
-            out_se[j, e, lanes(0)] = real
-            out_se[j, e, lanes(1)] = imag
-
-    others = landed.at[:, pl.ds(0, energies - 1)]
-    fewer = landed.at[:, pl.ds(0, energies - 2)]
-
-    @pl.when(jnp.logical_not(hosted))
-    def _():
-        pltpu.make_async_copy(others, others, swap_send.at[0]).wait()
-
-    @pl.when(first & (space < stages - 1))
-    def _():
-        sent(size - piece)
-        if not paired:
-            sent(piece, 1)
-
-    if paired:
-        @pl.when(first & middle)
-        def _():
-            sent(piece, 1)
-
-        @pl.when(hosted)
-        def _():
-            bring().wait_send()
-
-        @pl.when(gives)
-        def _():
-            aheads().wait_send()
-
-        @pl.when(second & (space == 0) & (stages > 1))
-        def _():
-            sent(size)
-
-        @pl.when(hosts)
-        def _():
-            pltpu.make_async_copy(fewer, fewer, swap_send.at[0]).wait()
-            copy(passed, g, (chain_send.at[0], chain_recv.at[0]), space, partner).wait_send()
-
-        @pl.when(links)
-        def _():
-            sent(size)
-
-        @pl.when(leaps)
-        def _():
-            sent(size)
-
-
-def write_out(g, se, out_g, out_se, sems):
-    copies = [
-        pltpu.make_async_copy(g, out_g.at[:, 0], sems.at[0]),
-        pltpu.make_async_copy(se, out_se, sems.at[1]),
-    ]
-    for copy in copies:
-        copy.start()
-    for copy in copies:
-        copy.wait()
+            se[j, e, lanes(0)] = real
+            se[j, e, lanes(1)] = imag
+        pltpu.make_async_copy(se.at[j], out_se.at[j], sems.at[1]).start()
+    pltpu.make_async_copy(g, out_g.at[:, 0], sems.at[0]).wait()
+    pltpu.make_async_copy(se, out_se, sems.at[1]).wait()
 
 
 def body(retain, hopping, source, screened):
@@ -654,20 +663,22 @@
     any_spec = pl.BlockSpec(memory_space=pl.ANY)
     vmem_spec = pl.BlockSpec(memory_space=pltpu.VMEM)
     vmem = pltpu.VMEM
-    greens, self_energy = pl.pallas_call(
+    greens, landed, kept = pl.pallas_call(
         kernel,
-        out_shape=(vmem((slabs, 2, size, size), F32), vmem(woven.shape, F32)),
+        out_shape=(
+            vmem((slabs, 2, size, size), F32),
+            vmem((slabs, energies, 2, rows, size), F32),
+            vmem(woven.shape, F32),
+        ),
         in_specs=[pl.BlockSpec(memory_space=pltpu.HBM)] * 4,
-        out_specs=(vmem_spec, vmem_spec),
+        out_specs=(vmem_spec,) * 3,
         scratch_shapes=[
             pltpu.SMEM((slabs,), F32),
             vmem((2, slabs, 2, size, size), F32),
-            vmem(woven.shape, F32),
             vmem((2 * slabs, OUTS, 4 * size // OUTS, 2 * size), BF16),
             vmem((2 * slabs, 2, 2 * size, 2 * size), BF16),
             vmem((slabs, 2 * size, size), F32),
             vmem((2, size, size), F32),
-            vmem((slabs, energies, 2, rows, size), F32),
             vmem((2 * slabs, 2 * size, size), F32),
             vmem((2 * slabs, 2 * size, size), F32),
             vmem((2, 2 * size, size), F32),
@@ -694,11 +705,11 @@
             jax.ShapeDtypeStruct(source.shape, F32),
             jax.ShapeDtypeStruct(woven.shape, F32),
         ),
-        in_specs=[vmem_spec, vmem_spec],
+        in_specs=[vmem_spec] * 3,
         out_specs=(any_spec, any_spec),
-        scratch_shapes=[pltpu.SemaphoreType.DMA((2,))],
+        scratch_shapes=[vmem(woven.shape, F32), pltpu.SemaphoreType.DMA((2,))],
         compiler_params=pltpu.CompilerParams(vmem_limit_bytes=4 << 20),
-    )(greens, self_energy)
+    )(greens, landed, kept)
     return greens, (
         self_energy.reshape(slabs, energies, rows, 2, size)
         .transpose(0, 1, 3, 2, 4)

time: 16.4 us -> 16.2 us (0.988)
  Pallas kernels: 15.6 us -> 15.4 us
    pallas_call x1, Pallas kernels: 14.8 us -> 14.6 us  [body(): pl.pallas_call(kernel, out_shape=(vmem((slabs, 2, size, size), F32), vmem...]
where the time goes in v5:
time: 16.2 us; the launch traced here: 16 us
  Pallas kernels  15.4 us (95%)
  between operations  0.64 us (4%)
    pallas_call x1, Pallas kernels, body(): pl.pallas_call(kernel, out_shape=(vmem((slabs, 2, size, size), F32), vmem...  14.6 us
    pallas_call x1, Pallas kernels, body(): pl.pallas_call(write_out, out_shape=(jax.ShapeDtypeStruct(source.shape, F...  0.83 us

profile of v5, /device:TPU:17, one launch (start us, length us, event | category | flops | bytes accessed | tf_op | source)
XLA Modules:
  0.0 16.0 jit_solution(12290058438919708151)
XLA Ops:
  0.6 14.6 %shard_map.59 = (f32[2,2,128,128]{3,2,1,0:T(8,128)S(1)}, f32[2,8,2,16,128]{4,3,2,1,0:T(8,128)S(1)}, f32[2,8,32,128]{3,2,1,0:T(8,128)S(1)}) custom-call(f32[2]{0:T(128)} %bitcast.12, f32[2,1,2,128,128]{4,3,2,1,0:T(8,128)} %hop_hbm.1, f32[2,1,2,128,128]{4,3,2,1,0:T(8,128)} %src_hbm.1, f32[2,8,32,128]{3,2,1,0:T(8,128)} %bitcast.11), custom_call_target="tpu_custom_call" | custom-call | tf_op jit(solution)/shard_map/pallas_call | solution.py:666
  15.2 0.8 %shard_map.60 = (f32[2,1,2,128,128]{4,3,2,1,0:T(8,128)}, f32[2,8,32,128]{3,2,1,0:T(8,128)}) custom-call(f32[2,2,128,128]{3,2,1,0:T(8,128)S(1)} %get-tuple-element.7.g, f32[2,8,2,16,128]{4,3,2,1,0:T(8,128)S(1)} %get-tuple-element.8.landed, f32[2,8,32,128]{3,2,1,0:T(8,128)S(1)} %get-tuple-element.9.scr), custom_call_target="tpu_custom_call" | custom-call | tf_op jit(solution)/shard_map/pallas_call | solution.py:702

commit v6 on v5

--- a/solution.py
+++ b/solution.py
@@ -630,6 +630,7 @@
 
 def write_out(g, landed, scr, out_g, out_se, se, sems):
     slabs, energies, _, rows, size = landed.shape
+    span = energies // 4 if energies % 4 == 0 else energies
 
     def lanes(part):
         return pl.ds(part, rows, stride=2)
@@ -646,7 +647,9 @@
                 imag = imag + (gr * si + gi * sr)
             se[j, e, lanes(0)] = real
             se[j, e, lanes(1)] = imag
-        pltpu.make_async_copy(se.at[j], out_se.at[j], sems.at[1]).start()
+            if (e + 1) % span == 0:
+                part = pl.ds(e + 1 - span, span)
+                pltpu.make_async_copy(se.at[j, part], out_se.at[j, part], sems.at[1]).start()
     pltpu.make_async_copy(g, out_g.at[:, 0], sems.at[0]).wait()
     pltpu.make_async_copy(se, out_se, sems.at[1]).wait()
 

time: 16.2 us -> 16.1 us (level)
  no operation moved by 1% of the time
where the time goes in v6:
time: 16.1 us; the launch traced here: 16 us
  Pallas kernels  15.4 us (96%)
  between operations  0.64 us (4%)
    pallas_call x1, Pallas kernels, body(): pl.pallas_call(kernel, out_shape=(vmem((slabs, 2, size, size), F32), vmem...  14.6 us
    pallas_call x1, Pallas kernels, body(): pl.pallas_call(write_out, out_shape=(jax.ShapeDtypeStruct(source.shape, F...  0.79 us

profile of v6, /device:TPU:17, one launch (start us, length us, event | category | flops | bytes accessed | tf_op | source)
XLA Modules:
  0.0 16.0 jit_solution(9181010682610725229)
XLA Ops:
  0.6 14.6 %shard_map.59 = (f32[2,2,128,128]{3,2,1,0:T(8,128)S(1)}, f32[2,8,2,16,128]{4,3,2,1,0:T(8,128)S(1)}, f32[2,8,32,128]{3,2,1,0:T(8,128)S(1)}) custom-call(f32[2]{0:T(128)} %bitcast.12, f32[2,1,2,128,128]{4,3,2,1,0:T(8,128)} %hop_hbm.1, f32[2,1,2,128,128]{4,3,2,1,0:T(8,128)} %src_hbm.1, f32[2,8,32,128]{3,2,1,0:T(8,128)} %bitcast.11), custom_call_target="tpu_custom_call" | custom-call | tf_op jit(solution)/shard_map/pallas_call | solution.py:669
  15.2 0.8 %shard_map.60 = (f32[2,1,2,128,128]{4,3,2,1,0:T(8,128)}, f32[2,8,32,128]{3,2,1,0:T(8,128)}) custom-call(f32[2,2,128,128]{3,2,1,0:T(8,128)S(1)} %get-tuple-element.7.g, f32[2,8,2,16,128]{4,3,2,1,0:T(8,128)S(1)} %get-tuple-element.8.landed, f32[2,8,32,128]{3,2,1,0:T(8,128)S(1)} %get-tuple-element.9.scr), custom_call_target="tpu_custom_call" | custom-call | tf_op jit(solution)/shard_map/pallas_call | solution.py:705

commit v7 on v6

--- a/solution.py
+++ b/solution.py
@@ -125,12 +125,12 @@
     leaps = links & (space + 2 < stages)
 
     loads = [
-        pltpu.make_async_copy(retain_hbm, retain, load_sem.at[2]),
+        pltpu.make_async_copy(retain_hbm, retain, swap_send.at[0]),
         *(
             pltpu.make_async_copy(
                 array.at[which, 0, part, pl.ds(i * size // LS, size // LS)],
                 ref.at[which, part, pl.ds(i * size // LS, size // LS)],
-                load_sem.at[0],
+                chain_send.at[0],
             )
             for array, ref, which in (
                 (hop_hbm, hop, slice(1, None)),
@@ -139,9 +139,9 @@
             for part in range(2)
             for i in range(LS)
         ),
-        pltpu.make_async_copy(src_hbm.at[1:, 0], src.at[1:], load_sem.at[3]),
-        pltpu.make_async_copy(hop_hbm.at[:1, 0], hop.at[:1], load_sem.at[3]),
-        pltpu.make_async_copy(scr_hbm, scr, load_sem.at[1]),
+        pltpu.make_async_copy(src_hbm.at[1:, 0], src.at[1:], chain_send.at[1]),
+        pltpu.make_async_copy(hop_hbm.at[:1, 0], hop.at[:1], chain_send.at[1]),
+        pltpu.make_async_copy(scr_hbm, scr, load_sem.at[0]),
     ]
     for load in loads:
         load.start()
@@ -204,10 +204,10 @@
         call(1)
 
     loads[0].wait()
-    pltpu.make_async_copy(hop, hop, load_sem.at[0]).wait()
+    pltpu.make_async_copy(hop, hop, chain_send.at[0]).wait()
 
     def settle():
-        pltpu.make_async_copy(hop, hop, load_sem.at[3]).wait()
+        pltpu.make_async_copy(hop, hop, chain_send.at[1]).wait()
 
     eye = (
         lax.broadcasted_iota(jnp.int32, (size, size), 0)
@@ -688,7 +688,7 @@
             vmem((2, size, size), F32),
             vmem((slabs, 2, size, size), F32),
             vmem((2 * slabs, size, 2 * size), F32),
-            pltpu.SemaphoreType.DMA((4,)),
+            pltpu.SemaphoreType.DMA((1,)),
             pltpu.SemaphoreType.DMA((2,)),
             pltpu.SemaphoreType.DMA((GROUPS,)),
             pltpu.SemaphoreType.DMA((GROUPS,)),

time: 16.1 us -> 16.1 us (level)
  no operation moved by 1% of the time
where the time goes in v7:
time: 16.1 us; the launch traced here: 15.9 us
  Pallas kernels  15.3 us (95%)
  between operations  0.64 us (4%)
    pallas_call x1, Pallas kernels, body(): pl.pallas_call(kernel, out_shape=(vmem((slabs, 2, size, size), F32), vmem...  14.5 us
    pallas_call x1, Pallas kernels, body(): pl.pallas_call(write_out, out_shape=(jax.ShapeDtypeStruct(source.shape, F...  0.79 us

profile of v7, /device:TPU:17, one launch (start us, length us, event | category | flops | bytes accessed | tf_op | source)
XLA Modules:
  0.0 15.9 jit_solution(4886538871874980261)
XLA Ops:
  0.6 14.5 %shard_map.59 = (f32[2,2,128,128]{3,2,1,0:T(8,128)S(1)}, f32[2,8,2,16,128]{4,3,2,1,0:T(8,128)S(1)}, f32[2,8,32,128]{3,2,1,0:T(8,128)S(1)}) custom-call(f32[2]{0:T(128)} %bitcast.12, f32[2,1,2,128,128]{4,3,2,1,0:T(8,128)} %hop_hbm.1, f32[2,1,2,128,128]{4,3,2,1,0:T(8,128)} %src_hbm.1, f32[2,8,32,128]{3,2,1,0:T(8,128)} %bitcast.11), custom_call_target="tpu_custom_call" | custom-call | tf_op jit(solution)/shard_map/pallas_call | solution.py:669
  15.2 0.8 %shard_map.60 = (f32[2,1,2,128,128]{4,3,2,1,0:T(8,128)}, f32[2,8,32,128]{3,2,1,0:T(8,128)}) custom-call(f32[2,2,128,128]{3,2,1,0:T(8,128)S(1)} %get-tuple-element.7.g, f32[2,8,2,16,128]{4,3,2,1,0:T(8,128)S(1)} %get-tuple-element.8.landed, f32[2,8,32,128]{3,2,1,0:T(8,128)S(1)} %get-tuple-element.9.scr), custom_call_target="tpu_custom_call" | custom-call | tf_op jit(solution)/shard_map/pallas_call | solution.py:705

commit v8 on v7

--- a/solution.py
+++ b/solution.py
@@ -278,7 +278,7 @@
         return copy(
             (g if source is None else source).at[j, :, rows_of],
             landed.at[j, energy if who is None else who],
-            (swap_send.at[0], swap_recv.at[j]),
+            (swap_send.at[0], swap_recv.at[0]),
             space,
             peer,
         )
@@ -576,13 +576,13 @@
 
     loads[-1].wait()
     mine = pl.ds(pl.multiple_of(energy * rows, rows), rows)
-    for j in range(last, -1, -1):
+    for j in range(slabs):
         landed[j, energy] = g[j, :, mine]
-        for count, there in ((energies - 2, hosts), (energies - 1, jnp.logical_not(hosts))):
-            @pl.when(there)
-            def _():
-                others = landed.at[j, pl.ds(0, count)]
-                pltpu.make_async_copy(others, others, swap_recv.at[j]).wait()
+    for count, there in ((energies - 2, hosts), (energies - 1, jnp.logical_not(hosts))):
+        @pl.when(there)
+        def _():
+            others = landed.at[:, pl.ds(0, count)]
+            pltpu.make_async_copy(others, others, swap_recv.at[0]).wait()
 
     others = landed.at[:, pl.ds(0, energies - 1)]
     fewer = landed.at[:, pl.ds(0, energies - 2)]
@@ -693,7 +693,7 @@
             pltpu.SemaphoreType.DMA((GROUPS,)),
             pltpu.SemaphoreType.DMA((GROUPS,)),
             pltpu.SemaphoreType.DMA((1,)),
-            pltpu.SemaphoreType.DMA((slabs,)),
+            pltpu.SemaphoreType.DMA((1,)),
             pltpu.SemaphoreType.DMA((3,)),
             pltpu.SemaphoreType.REGULAR,
             pltpu.SemaphoreType.REGULAR((max(energies.bit_length() - 2, 1),)),

time: 16.1 us -> 16.1 us (level)
  no operation moved by 1% of the time
where the time goes in v8:
time: 16.1 us; the launch traced here: 15.9 us
  Pallas kernels  15.3 us (95%)
  between operations  0.64 us (4%)
    pallas_call x1, Pallas kernels, body(): pl.pallas_call(kernel, out_shape=(vmem((slabs, 2, size, size), F32), vmem...  14.5 us
    pallas_call x1, Pallas kernels, body(): pl.pallas_call(write_out, out_shape=(jax.ShapeDtypeStruct(source.shape, F...  0.79 us

profile of v8, /device:TPU:17, one launch (start us, length us, event | category | flops | bytes accessed | tf_op | source)
XLA Modules:
  0.0 15.9 jit_solution(15534473350784095753)
XLA Ops:
  0.6 14.5 %shard_map.59 = (f32[2,2,128,128]{3,2,1,0:T(8,128)S(1)}, f32[2,8,2,16,128]{4,3,2,1,0:T(8,128)S(1)}, f32[2,8,32,128]{3,2,1,0:T(8,128)S(1)}) custom-call(f32[2]{0:T(128)} %bitcast.12, f32[2,1,2,128,128]{4,3,2,1,0:T(8,128)} %hop_hbm.1, f32[2,1,2,128,128]{4,3,2,1,0:T(8,128)} %src_hbm.1, f32[2,8,32,128]{3,2,1,0:T(8,128)} %bitcast.11), custom_call_target="tpu_custom_call" | custom-call | tf_op jit(solution)/shard_map/pallas_call | solution.py:669
  15.1 0.8 %shard_map.60 = (f32[2,1,2,128,128]{4,3,2,1,0:T(8,128)}, f32[2,8,32,128]{3,2,1,0:T(8,128)}) custom-call(f32[2,2,128,128]{3,2,1,0:T(8,128)S(1)} %get-tuple-element.7.g, f32[2,8,2,16,128]{4,3,2,1,0:T(8,128)S(1)} %get-tuple-element.8.landed, f32[2,8,32,128]{3,2,1,0:T(8,128)S(1)} %get-tuple-element.9.scr), custom_call_target="tpu_custom_call" | custom-call | tf_op jit(solution)/shard_map/pallas_call | solution.py:705
